TPU v7x, 32 devices: a whole 2x2x4 slice. The times are simulated.
32 devices in a mesh: group: 4 (over y, x), dev: 8 (over z, core).
Axes of the slice: x: 2, y: 2, z: 4, core: 2. Of those that a mesh axis runs over, the one named last changes fastest.
Arguments:
- density: float32 [32, 320, 128], P(('group', 'dev')), may hold values from 0.5 to 2
- velocity: float32 [3, 32, 320, 128], P(None, ('group', 'dev')), may hold values from -0.75 to 0.75
- pressure: float32 [32, 320, 128], P(('group', 'dev')), may hold values from 0.5 to 2
- rbf_blocks: bfloat16 [2048, 128, 128], P(('group', 'dev')), may hold values from -0.5 to 0.5
- correlation: int32 [2048, 128], P(('group', 'dev')), may hold values from 0 to 319
- normals: float32 [2048, 3, 128], P(('group', 'dev')), may hold values from -6 to 6
- routes: int32 [2048, 1], P(('group', 'dev')), may hold values from 0 to 31; in each aligned block of 64 rows (0 to 63, 64 to 127, ...) at most 4 rows name the same one
- targets: int32 [2048], P(('group', 'dev')), may hold values from 0 to 31
- stiffness: bfloat16 [1024, 128, 128], P(('group', 'dev')), may hold values from -0.35 to 2.35
- coupling: bfloat16 [1024, 128, 128], P(('group', 'dev')), may hold values from -0.5 to 0.5
- inverse_diag: float32 [1024, 3, 128], P(('group', 'dev')), may hold values from 0.5 to 1.5
- displacement: float32 [1024, 3, 128], P(('group', 'dev')), may hold values from -6 to 6
- diff_res: float32 [8, 1024, 3, 128], P(None, ('group', 'dev')), may hold values from -2 to 2
- diff_disp: float32 [8, 1024, 3, 128], P(None, ('group', 'dev')), may hold values from -2.4 to 2.4
Outputs:
- fluid_next: float32 [5, 32, 320, 128], P(None, ('group', 'dev'))
- disp_next: float32 [1024, 3, 128], P(('group', 'dev'))
- wall_motion: float32 [2048, 3, 128], P(('group', 'dev'))
Inputs may be any that keep to these rules, and one draw needn't show every extreme that they name: `routes`: among the 64 blocks of one device at most 4 name the same owner, and some device names one owner exactly 4 times.
All inputs are finite; a program needn't handle non-finite values.
Results may differ from a plain program's by a relative error of at most 0.0004.
The roundings to bfloat16 on the way count: a program that leaves them out, or rounds other values in their place, can miss the bound.
Values may be sent and summed in bfloat16 or wider, within the bound.
A program may use at most 64 MiB of HBM per device.

v0:
```python
import jax
import jax.numpy as jnp
from jax import lax
from jax.sharding import PartitionSpec as P

ratio_heat = 1.4
step_ratio = 0.03


def extended(value, sides, width):
    for axis, dim in sides:
        peers, length = (lax.axis_size(axis), value.shape[dim])
        up = [(i, (i + 1) % peers) for i in range(peers)]
        down = [(j, i) for i, j in up]
        last = lax.slice_in_dim(value, length - width, length, axis=dim)
        leading = lax.slice_in_dim(value, 0, width, axis=dim)
        before = lax.ppermute(last, axis, up)
        after = lax.ppermute(leading, axis, down)
        value = jnp.concatenate([before, value, after], axis=dim)
    return value


def shifted(block, axis, distance):
    devices = range(lax.axis_size(axis))
    route = [(i - distance, i) for i in devices if i - distance in devices]
    return lax.ppermute(block, axis, route)


def euler_flux(state, normal_axis):
    dens = state[0]
    vel = state[1:4] / dens
    press = (ratio_heat - 1.0) * (state[4] - 0.5 * dens * jnp.sum(vel * vel, axis=0))
    normal_speed = vel[normal_axis]
    rows = [dens * normal_speed]
    for comp in range(3):
        moment = state[1 + comp] * normal_speed
        if comp == normal_axis:
            moment = moment + press
        rows.append(moment)
    rows.append((state[4] + press) * normal_speed)
    wave_speed = jnp.abs(normal_speed) + jnp.sqrt(ratio_heat * press / dens)
    return (jnp.stack(rows, axis=0), wave_speed)


def rusanov(left_state, right_state, normal_axis):
    flux_left, speed_left = euler_flux(left_state, normal_axis)
    flux_right, speed_right = euler_flux(right_state, normal_axis)
    return 0.5 * (flux_left + flux_right) - 0.5 * jnp.maximum(speed_left, speed_right) * (
        right_state - left_state
    )


def conserve(density, velocity, pressure):
    energy = pressure / (ratio_heat - 1.0) + 0.5 * density * jnp.sum(velocity * velocity, axis=0)
    return jnp.concatenate([density[None], density[None] * velocity, energy[None]], axis=0)


def advance(padded, conserved):
    face_x = rusanov(padded[:, :-1], padded[:, 1:], 0)
    divergence = face_x[:, 1:] - face_x[:, :-1]
    face_y = rusanov(conserved, jnp.roll(conserved, -1, axis=2), 1)
    divergence = divergence + face_y - jnp.roll(face_y, 1, axis=2)
    mirror_sign = jnp.array([1.0, 1.0, 1.0, -1.0, 1.0], dtype=conserved.dtype)[:, None, None, None]
    padded_z = jnp.concatenate(
        [conserved[..., :1] * mirror_sign, conserved, conserved[..., -1:]], axis=3
    )
    face_z = rusanov(padded_z[..., :-1], padded_z[..., 1:], 2)
    divergence = divergence + face_z[..., 1:] - face_z[..., :-1]
    return conserved - step_ratio * divergence


def wall_pressure(state):
    bottom = state[..., 0]
    return (ratio_heat - 1.0) * (
        bottom[4] - 0.5 * jnp.sum(bottom[1:4] * bottom[1:4], axis=0) / bottom[0]
    )


def cho_apply(gram, projected):
    factor = jnp.linalg.cholesky(gram)
    middle = lax.linalg.triangular_solve(factor, projected[:, None], left_side=True, lower=True)
    return lax.linalg.triangular_solve(
        factor, middle, left_side=True, lower=True, transpose_a=True
    )[:, 0]


def on_device(
    density,
    velocity,
    pressure,
    rbf_blocks,
    correlation,
    normals,
    routes,
    targets,
    stiffness,
    coupling,
    inverse_diag,
    displacement,
    diff_res,
    diff_disp,
):
    conserved = conserve(density, velocity, pressure)
    padded = extended(conserved, ((("group", "dev"), 1),), 1)
    fluid_next = advance(padded, conserved)
    wall_row = wall_pressure(fluid_next).reshape(-1)
    weighted = (wall_row[correlation][:, None, :] * normals).astype(jnp.bfloat16)
    block_loads = jnp.einsum(
        "bci,bij->bcj", weighted, rbf_blocks, preferred_element_type=jnp.float32
    )
    blocks = block_loads.shape[0]
    width_row = block_loads.shape[1] * block_loads.shape[2]
    peer_count = lax.axis_size(("group", "dev"))
    capacity = max(2, 2 * blocks // peer_count)
    slot_count = peer_count * capacity
    target_dev = routes[:, 0]
    member = (target_dev[:, None] == jnp.arange(peer_count, dtype=jnp.int32)[None, :]).astype(
        jnp.int32
    )
    position = jnp.sum((jnp.cumsum(member, axis=0) - member) * member, axis=1)
    slot_id = target_dev * capacity + position
    send_loads = (
        jnp.zeros((slot_count, width_row), jnp.float32)
        .at[slot_id]
        .set(block_loads.reshape(blocks, width_row))
    )
    send_tag = (
        jnp.full((slot_count,), -1.0, jnp.float32).at[slot_id].set(targets.astype(jnp.float32))
    )
    got_loads, got_tag = (
        lax.all_to_all(
            send_loads.reshape(peer_count, capacity, width_row),
            ("group", "dev"),
            split_axis=0,
            concat_axis=0,
            tiled=True,
        ),
        lax.all_to_all(
            send_tag.reshape(peer_count, capacity),
            ("group", "dev"),
            split_axis=0,
            concat_axis=0,
            tiled=True,
        ),
    )
    got_loads = got_loads.reshape(slot_count, width_row)
    got_tag = got_tag.reshape(slot_count)
    solid_count = displacement.shape[0]
    selector = (got_tag[None, :] == jnp.arange(solid_count, dtype=jnp.float32)[:, None]).astype(
        jnp.float32
    )
    solid_load = jnp.dot(
        selector, got_loads, precision=lax.Precision.HIGHEST, preferred_element_type=jnp.float32
    ).reshape(displacement.shape)
    disp_half = displacement.astype(jnp.bfloat16)
    prior_block = shifted(disp_half[-1:], ("group", "dev"), 1)
    earlier = jnp.concatenate([prior_block, disp_half[:-1]], axis=0)
    solid_res = jnp.einsum("bcj,bij->bci", disp_half, stiffness, preferred_element_type=jnp.float32)
    solid_res = (
        solid_res
        + jnp.einsum("bcj,bij->bci", earlier, coupling, preferred_element_type=jnp.float32)
        - solid_load
    )
    coupling_res = -inverse_diag * solid_res
    projected_local = jnp.einsum(
        "mbcj,bcj->m", diff_res, coupling_res, precision=lax.Precision.HIGHEST
    )
    gram_local = jnp.einsum("mbcj,nbcj->mn", diff_res, diff_res, precision=lax.Precision.HIGHEST)
    gram_matrix, projected = lax.psum((gram_local, projected_local), ("group", "dev"))
    mixing = -cho_apply(gram_matrix, projected)
    disp_next = (
        displacement
        + coupling_res
        + jnp.einsum("mbcj,m->bcj", diff_disp, mixing, precision=lax.Precision.HIGHEST)
    )
    reply_rows = disp_next.astype(jnp.bfloat16).reshape(solid_count, width_row)
    replies = jnp.dot(
        selector.T.astype(jnp.bfloat16), reply_rows, preferred_element_type=jnp.float32
    ).astype(jnp.bfloat16)
    returned = lax.all_to_all(
        replies.reshape(peer_count, capacity, width_row),
        ("group", "dev"),
        split_axis=0,
        concat_axis=0,
        tiled=True,
    )
    picked = returned.reshape(slot_count, width_row)[slot_id].reshape(block_loads.shape)
    wall_motion = jnp.einsum("bij,bcj->bci", rbf_blocks, picked, preferred_element_type=jnp.float32)
    return (fluid_next, disp_next, wall_motion)


def solution(mesh):
    placed = (
        P(("group", "dev"), None, None),
        P(None, ("group", "dev"), None, None),
        P(("group", "dev"), None, None),
        P(("group", "dev"), None, None),
        P(("group", "dev"), None),
        P(("group", "dev"), None, None),
        P(("group", "dev"), None),
        P(("group", "dev")),
        P(("group", "dev"), None, None),
        P(("group", "dev"), None, None),
        P(("group", "dev"), None, None),
        P(("group", "dev"), None, None),
        P(None, ("group", "dev"), None, None),
        P(None, ("group", "dev"), None, None),
    )
    return jax.shard_map(
        on_device,
        mesh=mesh,
        in_specs=placed,
        out_specs=(
            P(None, ("group", "dev"), None, None),
            P(("group", "dev"), None, None),
            P(("group", "dev"), None, None),
        ),
        check_vma=False,
    )
```

profile of v0, /device:TPU:0, one launch (start us, length us, event | category | flops | bytes accessed | tf_op | source)
XLA Modules:
  0.0 170.8 jit_solution(8857625696449889218)
XLA Ops:
  0.7 1.4 multiply_reduce_fusion.5
  2.0 0.7 bitcast_dynamic-update-slice_fusion.1
  2.8 0.7 fusion.55
  3.4 0.7 fusion.54
  4.2 0.9 pad_maximum_fusion.3
  5.1 6.4 %collective-permute-start.1 = (f32[5,1,320,128]{3,2,1,0:T(8,128)}, f32[5,1,320,128]{3,2,1,0:T(8,128)}, u32[]{:S(2)}, u32[]{:S(2)}) collective-permute-start(f32[5,1,320,128]{3,2,1,0:T(8,128)} %pad_maximum_fusion.3), channel_id=1, source_target_pairs={{1,0},{2,1},{3,2},{4,3},{5,4},{6,5},{7,6},{8,7},{9,8},{10,9},{11,1... | collective-permute-start | bytes 2457608 | tf_op jit(solution)/shard_map/ppermute | solution.py:18
  11.7 0.2 select_reduce_fusion
  11.9 0.8 scatter_custom_fusion
  12.7 0.7 all_to_all.12
  13.4 5.7 %all-to-all-start = ((f32[32,1,4]{2,1,0:T(1,128)}), f32[32,1,4]{2,1,0:T(1,128)S(1)}, u32[]{:S(2)}, u32[]{:S(2)}) async-start(f32[32,1,4]{2,1,0:T(1,128)} %bitcast.30), calls=%async_computation | async-start | bytes 32768 | tf_op jit(solution)/shard_map/all_to_all | solution.py:138
  19.1 0.7 slice.284
  19.8 1.2 slice.283
  21.1 1.7 fusion.107
  22.8 0.5 pad_maximum_fusion.2
  23.4 0.3 multiply_reduce_fusion
  23.8 0.4 multiply_bitcast_fusion
  24.4 0.7 fusion.50
  25.2 0.8 copy-done.4
  26.0 0.2 fusion.68
  26.3 0.8 bitcast_dynamic-update-slice_fusion
  27.1 1.4 fusion.6
  28.6 0.6 multiply_subtract_fusion
  29.2 2.4 %collective-permute-done = f32[5,1,320,128]{3,2,1,0:T(8,128)} collective-permute-done((f32[5,1,320,128]{3,2,1,0:T(8,128)}, f32[5,1,320,128]{3,2,1,0:T(8,128)}, u32[]{:S(2)}, u32[]{:S(2)}) %collective-permute-start) | collective-permute-done | bytes 819232 | tf_op jit(solution)/shard_map/ppermute | solution.py:17
  31.6 1.7 %pad_maximum_fusion.1 = (f32[5,2,320,128]{3,2,1,0:T(8,128)S(1)}, f32[5,2,320,128]{3,2,1,0:T(8,128)S(1)}) fusion(f32[5,1,320,128]{3,2,1,0:T(8,128)} %collective-permute-done.1, f32[1,1,320,128]{3,2,1,0:T(8,128)S(1)} %bitcast.216, f32[3,1,320,128]{3,2,1,0:T(8,128)S(1)} %get-tuple-element.48, f32[1,1,320,128]{3,2,1,0:T(8,128)S(1)} %bitcast.209, ...), kind=kLoop, calls=%fused_computation.12 | loop fusion | flops 2457600 | bytes 5734400 | tf_op jit(solution)/shard_map/concatenate | solution.py:19
  33.4 0.3 multiply_reduce_fusion.2
  33.7 0.4 multiply_bitcast_fusion.1
  34.6 1.7 %multiply_subtract_fusion.1 = f32[5,2,320,128]{3,2,1,0:T(8,128)S(1)} fusion(f32[5,2,320,128]{3,2,1,0:T(8,128)S(1)} %multiply_dynamic-update-slice_fusion.6, f32[5,2,320,128]{3,2,1,0:T(8,128)S(1)} %multiply_dynamic-update-slice_fusion.4, f32[2,320,128]{2,1,0:T(8,128)S(1)} %get-tuple-element.18, f32[5,1,320,128]{3,2,1,0:T(8,128)} %collective-permute-done.1, ...), kind=kLoop, calls=%fused_computation.16 | loop fusion | flops 4505600 | bytes 7700480 | tf_op jit(solution)/shard_map/sub | solution.py:48
  36.3 0.4 fusion.8
  36.7 0.2 slice_reduce_fusion
  36.9 0.2 fusion.13
  37.0 0.5 copy-done.2
  37.6 51.2 %gather_fusion = f32[8192]{0:T(1024)S(1)} fusion(f32[320]{0:T(512)S(1)} %subtract_multiply_fusion, s32[8192]{0:T(1024)S(1)} %fusion.78), kind=kCustom, calls=%fused_computation | custom fusion | bytes 98304 | tf_op jit(solution)/shard_map/gather | solution.py:107
  88.9 1.3 fusion.74
  90.2 1.8 %scatter_custom_fusion.1 = f32[128,384]{1,0:T(8,128)} fusion(s32[64]{0:T(128)} %copy-done.14, f32[8,8,3,128]{3,2,1,0:T(4,128)} %bitcast.223, f32[]{:T(128)} %constant.80.clone.1), kind=kCustom, calls=%fused_computation.164 | custom fusion | bytes 328192 | tf_op jit(solution)/shard_map/scatter | solution.py:125
  92.0 1.7 reshape.784
  93.7 3.6 %all-to-all-start.1 = ((f32[32,4,384]{2,1,0:T(4,128)}), f32[32,4,384]{2,1,0:T(4,128)}, u32[]{:S(2)}, u32[]{:S(2)}) async-start(f32[32,4,384]{2,1,0:T(4,128)} %reshape.784), calls=%async_computation.1 | async-start | bytes 393216 | tf_op jit(solution)/shard_map/all_to_all | solution.py:131
  97.2 0.8 copy.93
  98.1 0.5 slice.318
  98.6 2.7 %collective-permute-start.2 = (bf16[1,3,128]{2,1,0:T(4,128)(2,1)}, bf16[1,3,128]{2,1,0:T(4,128)(2,1)}, u32[]{:S(2)}, u32[]{:S(2)}) collective-permute-start(bf16[1,3,128]{2,1,0:T(4,128)(2,1)} %slice.318), channel_id=1, source_target_pairs={{0,1},{1,2},{2,3},{3,4},{4,5},{5,6},{6,7},{7,8},{8,9},{9,10},{10,1... | collective-permute-start | bytes 2312 | tf_op jit(solution)/shard_map/ppermute | solution.py:26
  101.3 0.6 slice.319
  101.9 1.6 convolution_bitcast_fusion
  103.5 1.3 fusion.108
  104.8 0.5 broadcast.289
  105.3 0.6 reduce.20
  106.1 1.0 reshape.785
  107.2 0.2 fusion.87
  107.4 1.9 %fusion.1 = f32[32,3,128]{2,1,0:T(4,128)S(1)} fusion(f32[32,3,128]{2,1,0:T(4,128)} %fusion.108, bf16[32,128,128]{2,1,0:T(8,128)(2,1)} %param.24, f32[32,3,128]{2,0,1:T(8,128)S(1)} %fusion.87, f32[32,3,128]{2,0,1:T(8,128)} %param.25, bf16[31,3,128]{2,1,0:T(4,128)(2,1)} %slice.319, bf16[1,3,128]{2,1,0:T(4,128)(2,1)} %collective-permute-done.2), kind=kOutput, calls=%fused_computation.20 | convolution fusion | flops 3244032 | bytes 1269760 | tf_op jit(solution)/shard_map/bcj,bij->bci/dot_general | solution.py:161
  109.4 1.1 convolution_bitcast_fusion.3
  110.5 40.0 %all-reduce = (f32[8,8]{0,1:T(8,128)S(1)}, f32[8]{0:T(128)S(1)}) all-reduce(f32[8,8]{0,1:T(8,128)S(1)} %copy-done.12, f32[8]{0:T(128)S(1)} %convolution_bitcast_fusion.3), channel_id=1, replica_groups=mesh['group'=4,'dev'=8] {'group','dev'}, use_global_device_ids=true, to_apply=%region_12.13 | all-reduce | flops 72 | bytes 576 | tf_op jit(solution)/shard_map/psum | solution.py:169
  150.6 0.7 cholesky.16
  151.4 0.6 compare_reduce_fusion
  152.0 0.6 fusion.90
  152.7 0.6 custom-call.8
  153.3 0.1 convolution_bitcast_fusion.2
  153.4 0.1 fusion.3
  153.6 0.7 fusion.14
  154.3 0.2 convolution_convert_fusion
  154.5 0.7 reshape.787
  155.2 5.3 %all-to-all-start.2 = ((bf16[32,4,384]{2,1,0:T(4,128)(2,1)}), bf16[32,4,384]{2,1,0:T(4,128)(2,1)S(1)}, u32[]{:S(2)}, u32[]{:S(2)}) async-start(bf16[32,4,384]{2,1,0:T(4,128)(2,1)} %reshape.787), calls=%async_computation.2 | async-start | bytes 196608 | tf_op jit(solution)/shard_map/all_to_all | solution.py:180
  160.5 0.6 copy.55
  161.1 7.1 %all-to-all-done.2 = bf16[32,4,384]{2,1,0:T(4,128)(2,1)S(1)} async-done(((bf16[32,4,384]{2,1,0:T(4,128)(2,1)}), bf16[32,4,384]{2,1,0:T(4,128)(2,1)S(1)}, u32[]{:S(2)}, u32[]{:S(2)}) %all-to-all-start.2) | async-done | bytes 98336 | tf_op jit(solution)/shard_map/all_to_all | solution.py:180
  168.3 0.7 gather_fusion.1
  169.0 1.2 fusion.109
  170.2 0.7 copy.56
  (82 shorter events, 2.0 us)
Async XLA Ops:
  0.6 88.2 %copy-start = (bf16[64,128,128]{2,1,0:T(8,128)(2,1)S(1)}, bf16[64,128,128]{2,1,0:T(8,128)(2,1)}, u32[]{:S(2)}) copy-start(bf16[64,128,128]{2,1,0:T(8,128)(2,1)} %param.18) | copy-start | bytes 6291460
  0.6 1.4 copy-start.1
  0.7 2.8 %copy-start.9 = (f32[1,320,128]{2,1,0:T(8,128)S(1)}, f32[1,320,128]{2,1,0:T(8,128)}, u32[]{:S(2)}) copy-start(f32[1,320,128]{2,1,0:T(8,128)} %param.17) | copy-start | bytes 491524
  2.0 3.1 %copy-start.3 = (f32[320,128]{1,0:T(8,128)}, f32[320,128]{1,0:T(8,128)S(1)}, u32[]{:S(2)}) copy-start(f32[320,128]{1,0:T(8,128)S(1)} %get-tuple-element.29) | copy-start | bytes 491524
  2.7 8.8 %copy-start.13 = (s32[64,1]{0,1:T(1,128)S(1)}, s32[64,1]{0,1:T(1,128)}, u32[]{:S(2)}) copy-start(s32[64,1]{0,1:T(1,128)} %param.21) | copy-start | bytes 772
  3.4 8.4 %copy-start.17 = (s32[64]{0:T(128)S(1)}, s32[64]{0:T(128)}, u32[]{:S(2)}) copy-start(s32[64]{0:T(128)} %param.22) | copy-start | bytes 772
  4.2 16.9 %copy-start.16 = (f32[5]{0:T(128)S(1)}, f32[5]{0:T(128)}, u32[]{:S(2)}) copy-start(f32[5]{0:T(128)} %constant.91.clone) | copy-start | bytes 64
  5.1 24.1 %collective-permute-start.1 = (f32[5,1,320,128]{3,2,1,0:T(8,128)}, f32[5,1,320,128]{3,2,1,0:T(8,128)}, u32[]{:S(2)}, u32[]{:S(2)}) collective-permute-start(f32[5,1,320,128]{3,2,1,0:T(8,128)} %pad_maximum_fusion.3), channel_id=1, source_target_pairs={{1,0},{2,1},{3,2},{4,3},{5,4},{6,5},{7,6},{8,7},{9,8},{10,9},{11,1... | collective-permute-start | bytes 2457608 | tf_op jit(solution)/shard_map/ppermute | solution.py:18
  11.5 20.1 %collective-permute-start = (f32[5,1,320,128]{3,2,1,0:T(8,128)}, f32[5,1,320,128]{3,2,1,0:T(8,128)}, u32[]{:S(2)}, u32[]{:S(2)}) collective-permute-start(f32[5,1,320,128]{3,2,1,0:T(8,128)} %pad_maximum_fusion.3), channel_id=1, source_target_pairs={{0,1},{1,2},{2,3},{3,4},{4,5},{5,6},{6,7},{7,8},{8,9},{9,10},{10,1... | collective-permute-start | bytes 2457608 | tf_op jit(solution)/shard_map/ppermute | solution.py:17
  11.9 10.9 %copy-start.14 = (s32[64]{0:T(128)}, s32[64]{0:T(128)S(1)}, u32[]{:S(2)}) copy-start(s32[64]{0:T(128)S(1)} %fusion.94) | copy-start | bytes 772
  13.4 80.2 %all-to-all-start = ((f32[32,1,4]{2,1,0:T(1,128)}), f32[32,1,4]{2,1,0:T(1,128)S(1)}, u32[]{:S(2)}, u32[]{:S(2)}) async-start(f32[32,1,4]{2,1,0:T(1,128)} %bitcast.30), calls=%async_computation | async-start | bytes 32768 | tf_op jit(solution)/shard_map/all_to_all | solution.py:138
  25.1 0.9 copy-start.4
  27.1 1.5 copy-start.11
  36.7 0.9 copy-start.2
  37.6 51.2 %copy-start.10 = (f32[64,3,128]{2,0,1:T(8,128)S(1)}, f32[64,3,128]{2,0,1:T(8,128)}, u32[]{:S(2)}) copy-start(f32[64,3,128]{2,0,1:T(8,128)} %param.20) | copy-start | bytes 294916
  88.9 13.1 %copy-start.5 = (f32[8,32,3,128]{3,1,2,0:T(8,128)S(1)}, f32[8,32,3,128]{3,1,2,0:T(8,128)}, u32[]{:S(2)}) copy-start(f32[8,32,3,128]{3,1,2,0:T(8,128)} %param.27) | copy-start | bytes 1179652
  88.9 14.6 %copy-start.6 = (bf16[32,128,128]{2,1,0:T(8,128)(2,1)S(1)}, bf16[32,128,128]{2,1,0:T(8,128)(2,1)}, u32[]{:S(2)}) copy-start(bf16[32,128,128]{2,1,0:T(8,128)(2,1)} %param.23) | copy-start | bytes 3145732
  93.7 12.4 %all-to-all-start.1 = ((f32[32,4,384]{2,1,0:T(4,128)}), f32[32,4,384]{2,1,0:T(4,128)}, u32[]{:S(2)}, u32[]{:S(2)}) async-start(f32[32,4,384]{2,1,0:T(4,128)} %reshape.784), calls=%async_computation.1 | async-start | bytes 393216 | tf_op jit(solution)/shard_map/all_to_all | solution.py:131
  98.6 8.8 %collective-permute-start.2 = (bf16[1,3,128]{2,1,0:T(4,128)(2,1)}, bf16[1,3,128]{2,1,0:T(4,128)(2,1)}, u32[]{:S(2)}, u32[]{:S(2)}) collective-permute-start(bf16[1,3,128]{2,1,0:T(4,128)(2,1)} %slice.318), channel_id=1, source_target_pairs={{0,1},{1,2},{2,3},{3,4},{4,5},{5,6},{6,7},{7,8},{8,9},{9,10},{10,1... | collective-permute-start | bytes 2312 | tf_op jit(solution)/shard_map/ppermute | solution.py:26
  104.8 5.7 %copy-start.12 = (f32[8,8]{0,1:T(8,128)S(1)}, f32[8,8]{0,1:T(8,128)}, u32[]{:S(2)}) copy-start(f32[8,8]{0,1:T(8,128)} %convolution_bitcast_fusion) | copy-start | bytes 772
  104.8 48.8 %copy-start.7 = (f32[8,32,3,128]{3,1,2,0:T(8,128)S(1)}, f32[8,32,3,128]{3,1,2,0:T(8,128)}, u32[]{:S(2)}) copy-start(f32[8,32,3,128]{3,1,2,0:T(8,128)} %param.28) | copy-start | bytes 1179652
  106.0 48.2 %copy-start.8 = (f32[32,3,128]{2,0,1:T(8,128)S(1)}, f32[32,3,128]{2,0,1:T(8,128)}, u32[]{:S(2)}) copy-start(f32[32,3,128]{2,0,1:T(8,128)} %param.26) | copy-start | bytes 147460
  107.2 53.3 %copy-start.15 = (s32[64]{0:T(128)S(1)}, s32[64]{0:T(128)}, u32[]{:S(2)}) copy-start(s32[64]{0:T(128)} %copy-done.14) | copy-start | bytes 772
  155.2 13.0 %all-to-all-start.2 = ((bf16[32,4,384]{2,1,0:T(4,128)(2,1)}), bf16[32,4,384]{2,1,0:T(4,128)(2,1)S(1)}, u32[]{:S(2)}, u32[]{:S(2)}) async-start(bf16[32,4,384]{2,1,0:T(4,128)(2,1)} %reshape.787), calls=%async_computation.2 | async-start | bytes 196608 | tf_op jit(solution)/shard_map/all_to_all | solution.py:180
where the time goes:
time: 172 us; the launch traced here: 171 us
  local copies, waits for them, and re-layouts  66.3 us (39%)
  blocking collectives  40 us (23%)
  starting transfers between devices  23.6 us (14%)
  other arithmetic  20.4 us (12%)
  matrix products  9.77 us (6%)
  waiting for transfers between devices  9.52 us (6%)
    gather x1, local copies, waits for them, and re-layouts, on_device(): wall_row[correlation][:, None, :] * normals  51.2 us
    psum x1, blocking collectives, on_device(): lax.psum((gram_local, projected_local), ('group', 'dev'))  40 us
    all_to_all x1, waiting for transfers between devices, on_device(): lax.all_to_all(replies.reshape(peer_count, capacity, width_row), ('group'...  7.1 us
    ppermute x1, starting transfers between devices, extended(): after = lax.ppermute(leading, axis, down)  6.4 us
    all_to_all x1, starting transfers between devices, on_device(): lax.all_to_all(send_tag.reshape(peer_count, capacity), ('group', 'dev'),...  5.7 us
    all_to_all x1, starting transfers between devices, on_device(): lax.all_to_all(replies.reshape(peer_count, capacity, width_row), ('group'...  5.25 us
    sub x3, other arithmetic, rusanov(): 0.5 * (flux_left + flux_right)  3.7 us
    all_to_all x1, starting transfers between devices, on_device(): lax.all_to_all(send_loads.reshape(peer_count, capacity, width_row), ('gro...  3.57 us
  transfers between devices with their start and end apart: 6, of which 2 were waited for; matrix products, arithmetic and copies ran while one was open for 47% of the time, Pallas kernels for 0%

commit v1 on v0

--- a/solution.py
+++ b/solution.py
@@ -1,6 +1,8 @@
 import jax
 import jax.numpy as jnp
 from jax import lax
+from jax.experimental import pallas as pl
+from jax.experimental.pallas import tpu as pltpu
 from jax.sharding import PartitionSpec as P
 
 ratio_heat = 1.4
@@ -74,6 +76,27 @@
     return (ratio_heat - 1.0) * (
         bottom[4] - 0.5 * jnp.sum(bottom[1:4] * bottom[1:4], axis=0) / bottom[0]
     )
+
+
+def wall_at_kernel(wall_ref, index_ref, out_ref):
+    index = index_ref[...]
+    lanes = index.shape[1]
+    low = index % lanes
+    result = jnp.zeros(index.shape, jnp.float32)
+    for row in range(wall_ref.shape[0]):
+        source = jnp.broadcast_to(wall_ref[row : row + 1, :], index.shape)
+        found = jnp.take_along_axis(source, low, axis=1)
+        result = jnp.where(index // lanes == row, found, result)
+    out_ref[...] = result
+
+
+def wall_at(wall_row, correlation):
+    lanes = correlation.shape[1]
+    rows = -(-wall_row.shape[0] // lanes)
+    table = jnp.pad(wall_row, (0, rows * lanes - wall_row.shape[0])).reshape(rows, lanes)
+    return pl.pallas_call(
+        wall_at_kernel, out_shape=jax.ShapeDtypeStruct(correlation.shape, jnp.float32)
+    )(table, correlation)
 
 
 def cho_apply(gram, projected):
@@ -104,7 +127,7 @@
     padded = extended(conserved, ((("group", "dev"), 1),), 1)
     fluid_next = advance(padded, conserved)
     wall_row = wall_pressure(fluid_next).reshape(-1)
-    weighted = (wall_row[correlation][:, None, :] * normals).astype(jnp.bfloat16)
+    weighted = (wall_at(wall_row, correlation)[:, None, :] * normals).astype(jnp.bfloat16)
     block_loads = jnp.einsum(
         "bci,bij->bcj", weighted, rbf_blocks, preferred_element_type=jnp.float32
     )
@@ -166,7 +189,18 @@
         "mbcj,bcj->m", diff_res, coupling_res, precision=lax.Precision.HIGHEST
     )
     gram_local = jnp.einsum("mbcj,nbcj->mn", diff_res, diff_res, precision=lax.Precision.HIGHEST)
-    gram_matrix, projected = lax.psum((gram_local, projected_local), ("group", "dev"))
+    columns = projected_local.shape[0]
+    stats = jnp.concatenate([gram_local.reshape(-1), projected_local])
+    everyone = lax.all_to_all(
+        jnp.broadcast_to(stats[None], (peer_count, stats.shape[0])),
+        ("group", "dev"),
+        split_axis=0,
+        concat_axis=0,
+        tiled=True,
+    )
+    totals = jnp.sum(everyone, axis=0)
+    gram_matrix = totals[: columns * columns].reshape(columns, columns)
+    projected = totals[columns * columns :]
     mixing = -cho_apply(gram_matrix, projected)
     disp_next = (
         displacement

time: 172 us -> 95.6 us (0.56)
  local copies, waits for them, and re-layouts: 66.3 us -> 17.4 us
  blocking collectives: 40 us -> 12.3 us
  starting transfers between devices: 23.6 us -> 20.9 us
    gather x1 -> x0, local copies, waits for them, and re-layouts: 51.2 us -> none  [on_device(): wall_row[correlation][:, None, :] * normals]
    psum x1 -> x0, blocking collectives: 40 us -> none  [on_device(): lax.psum((gram_local, projected_local), ('group', 'dev'))]
    all_to_all x0 -> x1, blocking collectives: none -> 12.3 us  [on_device(): lax.all_to_all(jnp.broadcast_to(stats[None], (peer_count, stats.shape[0])...]
    all_to_all x1, starting transfers between devices: 5.25 us -> 2.57 us  [on_device(): lax.all_to_all(replies.reshape(peer_count, capacity, width_row), ('group'...]
    reshape x0 -> x4, local copies, waits for them, and re-layouts: none -> 2.1 us  [the longest x1 1.34 us: on_device(): stats = jnp.concatenate([gram_local.reshape(-1), projected_local])]
  transfers between devices with their start and end apart: 6 -> 6, of which waited for: 2 -> 2; matrix products, arithmetic and copies ran while one was open for 47% -> 34% of each run, Pallas kernels for 0% -> 2%
where the time goes in v1:
time: 95.6 us; the launch traced here: 94.6 us
  other arithmetic  21.2 us (22%)
  starting transfers between devices  20.9 us (22%)
  local copies, waits for them, and re-layouts  17.4 us (18%)
  blocking collectives  12.3 us (13%)
  matrix products  10.6 us (11%)
  waiting for transfers between devices  9.55 us (10%)
  Pallas kernels  1.51 us (2%)
  between operations  1.17 us (1%)
    all_to_all x1, blocking collectives, on_device(): lax.all_to_all(jnp.broadcast_to(stats[None], (peer_count, stats.shape[0])...  12.3 us
    all_to_all x1, waiting for transfers between devices, on_device(): lax.all_to_all(replies.reshape(peer_count, capacity, width_row), ('group'...  7.1 us
    ppermute x1, starting transfers between devices, extended(): after = lax.ppermute(leading, axis, down)  6.4 us
    all_to_all x1, starting transfers between devices, on_device(): lax.all_to_all(send_tag.reshape(peer_count, capacity), ('group', 'dev'),...  5.7 us
    unnamed x39, local copies, waits for them, and re-layouts  3.7 us
    sub x3, other arithmetic, rusanov(): 0.5 * (flux_left + flux_right)  3.67 us
    unnamed x20, other arithmetic  3.54 us
    all_to_all x1, starting transfers between devices, on_device(): lax.all_to_all(send_loads.reshape(peer_count, capacity, width_row), ('gro...  3.54 us
  transfers between devices with their start and end apart: 6, of which 2 were waited for; matrix products, arithmetic and copies ran while one was open for 34% of the time, Pallas kernels for 2%

profile of v1, /device:TPU:0, one launch (start us, length us, event | category | flops | bytes accessed | tf_op | source)
XLA Modules:
  0.0 94.6 jit_solution(10915639869890050841)
XLA Ops:
  0.7 1.4 %multiply_reduce_fusion.5 = (f32[320,128]{1,0:T(8,128)S(1)}, f32[3,1,320,128]{3,2,1,0:T(8,128)S(1)}, f32[3,1,320,128]{3,2,1,0:T(8,128)S(1)}, f32[320,128]{1,0:T(8,128)S(1)}) fusion(f32[3,1,320,128]{3,2,1,0:T(8,128)} %param.16, f32[320,128]{1,0:T(8,128)} %bitcast.205), kind=kLoop, calls=%fused_computation.57 | loop fusion | flops 655360 | bytes 1966080 | tf_op jit(solution)/shard_map/reduce_sum | solution.py:34
  2.0 0.7 bitcast_dynamic-update-slice_fusion.1
  2.8 0.7 fusion.55
  3.4 0.7 fusion.54
  4.2 0.9 pad_maximum_fusion.3
  5.1 6.4 %collective-permute-start.1 = (f32[5,1,320,128]{3,2,1,0:T(8,128)}, f32[5,1,320,128]{3,2,1,0:T(8,128)}, u32[]{:S(2)}, u32[]{:S(2)}) collective-permute-start(f32[5,1,320,128]{3,2,1,0:T(8,128)} %pad_maximum_fusion.3), channel_id=1, source_target_pairs={{1,0},{2,1},{3,2},{4,3},{5,4},{6,5},{7,6},{8,7},{9,8},{10,9},{11,1... | collective-permute-start | bytes 2457608 | tf_op jit(solution)/shard_map/ppermute | solution.py:20
  11.7 0.2 select_reduce_fusion
  11.9 0.8 scatter_custom_fusion
  12.7 0.7 all_to_all.16
  13.4 5.7 %all-to-all-start = ((f32[32,1,4]{2,1,0:T(1,128)}), f32[32,1,4]{2,1,0:T(1,128)S(1)}, u32[]{:S(2)}, u32[]{:S(2)}) async-start(f32[32,1,4]{2,1,0:T(1,128)} %bitcast.30), calls=%async_computation | async-start | bytes 32768 | tf_op jit(solution)/shard_map/all_to_all | solution.py:161
  19.1 0.7 slice.298
  19.8 1.2 %slice.297 = f32[5,1,319,128]{3,2,1,0:T(8,128)S(1)} slice(f32[5,1,320,128]{3,2,1,0:T(8,128)} %pad_maximum_fusion.3), slice={[0:5], [0:1], [1:320], [0:128]} | slice | bytes 1633280 | tf_op jit(solution)/shard_map/jit(_roll_static)/slice | solution.py:63
  21.1 1.7 %fusion.106 = (f32[5,1,320,1]{3,2,1,0:T(8,128)S(1)}, f32[5,1,320,1]{3,2,1,0:T(8,128)S(1)}) fusion(f32[5,1,320,128]{3,2,1,0:T(8,128)} %pad_maximum_fusion.3, f32[5]{0:T(128)S(1)} %copy-done.16), kind=kLoop, calls=%fused_computation.213 | loop fusion | flops 1600 | bytes 25620 | tf_op jit(solution)/shard_map/slice | solution.py:67
  22.8 0.5 pad_maximum_fusion.2
  23.4 0.3 multiply_reduce_fusion
  23.8 0.4 multiply_bitcast_fusion
  24.4 0.7 fusion.50
  25.3 0.8 copy-done.4
  26.0 0.2 fusion.68
  26.3 0.8 bitcast_dynamic-update-slice_fusion
  27.1 1.4 %fusion.6 = f32[5,1,320,128]{3,2,1,0:T(8,128)S(1)} fusion(f32[5,1,1,128]{3,2,1,0:T(1,128)S(1)} %slice.298, f32[5,1,320,128]{3,2,1,0:T(8,128)} %get-tuple-element.56, f32[5,1,320,128]{3,2,1,0:T(8,128)S(1)} %get-tuple-element.57, f32[5,1,319,128]{3,2,1,0:T(8,128)S(1)} %slice.297, f32[320,128]{1,0:T(8,128)S(1)} %fusion.68, f32[1,1,320,128]{3,2,1,0:T(8,128)S(1)} %bitcast.215, ...), kind=kLoop, calls=%fused_computation.36 | loop fusion | flops 1638400 | bytes 4259840 | tf_op jit(solution)/shard_map/sub | solution.py:50
  28.6 0.6 multiply_subtract_fusion
  29.2 2.4 %collective-permute-done = f32[5,1,320,128]{3,2,1,0:T(8,128)} collective-permute-done((f32[5,1,320,128]{3,2,1,0:T(8,128)}, f32[5,1,320,128]{3,2,1,0:T(8,128)}, u32[]{:S(2)}, u32[]{:S(2)}) %collective-permute-start) | collective-permute-done | bytes 819232 | tf_op jit(solution)/shard_map/ppermute | solution.py:19
  31.6 1.7 %pad_maximum_fusion.1 = (f32[5,2,320,128]{3,2,1,0:T(8,128)S(1)}, f32[5,2,320,128]{3,2,1,0:T(8,128)S(1)}) fusion(f32[5,1,320,128]{3,2,1,0:T(8,128)} %collective-permute-done.1, f32[1,1,320,128]{3,2,1,0:T(8,128)S(1)} %bitcast.217, f32[3,1,320,128]{3,2,1,0:T(8,128)S(1)} %get-tuple-element.52, f32[1,1,320,128]{3,2,1,0:T(8,128)S(1)} %bitcast.210, ...), kind=kLoop, calls=%fused_computation.11 | loop fusion | flops 2457600 | bytes 5734400 | tf_op jit(solution)/shard_map/concatenate | solution.py:21
  33.4 0.3 multiply_reduce_fusion.2
  33.7 0.4 multiply_bitcast_fusion.1
  34.5 1.7 %multiply_subtract_fusion.1 = f32[5,2,320,128]{3,2,1,0:T(8,128)S(1)} fusion(f32[5,2,320,128]{3,2,1,0:T(8,128)S(1)} %multiply_dynamic-update-slice_fusion.6, f32[5,2,320,128]{3,2,1,0:T(8,128)S(1)} %multiply_dynamic-update-slice_fusion.4, f32[2,320,128]{2,1,0:T(8,128)S(1)} %get-tuple-element.22, f32[5,1,320,128]{3,2,1,0:T(8,128)} %collective-permute-done.1, ...), kind=kLoop, calls=%fused_computation.15 | loop fusion | flops 4505600 | bytes 7700480 | tf_op jit(solution)/shard_map/sub | solution.py:50
  36.2 0.4 fusion.8
  36.8 0.7 copy-done.2
  37.6 0.6 pad_bitcast_fusion.wall_ref
  38.3 1.5 %shard_map.166 = f32[64,128]{1,0:T(8,128)} custom-call(f32[3,128]{1,0:T(4,128)} %pad_bitcast_fusion.wall_ref, s32[64,128]{1,0:T(8,128)} %index_ref.1), custom_call_target="tpu_custom_call" | custom-call | tf_op jit(solution)/shard_map/pallas_call | solution.py:97
  39.8 0.8 multiply_convert_fusion
  40.6 1.3 %fusion.74 = f32[64,3,128]{2,1,0:T(4,128)} fusion(bf16[64,128,128]{2,1,0:T(8,128)(2,1)S(1)} %copy-done, bf16[64,3,128]{2,0,1:T(8,128)(2,1)S(1)} %multiply_convert_fusion), kind=kOutput, calls=%fused_computation.171 | convolution fusion | flops 6291456 | bytes 2244608 | tf_op jit(solution)/shard_map/bci,bij->bcj/dot_general | solution.py:131
  41.9 1.8 %scatter_custom_fusion.1 = f32[128,384]{1,0:T(8,128)} fusion(s32[64]{0:T(128)} %copy-done.13, f32[8,8,3,128]{3,2,1,0:T(4,128)} %bitcast.224, f32[]{:T(128)} %constant.79.clone.1), kind=kCustom, calls=%fused_computation.163 | custom fusion | bytes 328192 | tf_op jit(solution)/shard_map/scatter | solution.py:148
  43.7 1.7 %reshape.808 = f32[32,4,384]{2,1,0:T(4,128)} reshape(f32[128,384]{1,0:T(8,128)} %scatter_custom_fusion.1) | data formatting | bytes 393216 | tf_op jit(solution)/shard_map/reshape | solution.py:155
  45.4 3.5 %all-to-all-start.1 = ((f32[32,4,384]{2,1,0:T(4,128)}), f32[32,4,384]{2,1,0:T(4,128)}, u32[]{:S(2)}, u32[]{:S(2)}) async-start(f32[32,4,384]{2,1,0:T(4,128)} %reshape.808), calls=%async_computation.1 | async-start | bytes 393216 | tf_op jit(solution)/shard_map/all_to_all | solution.py:154
  48.9 0.8 copy.116
  49.8 0.6 slice.332
  50.4 2.7 %collective-permute-start.2 = (bf16[1,3,128]{2,1,0:T(4,128)(2,1)}, bf16[1,3,128]{2,1,0:T(4,128)(2,1)}, u32[]{:S(2)}, u32[]{:S(2)}) collective-permute-start(bf16[1,3,128]{2,1,0:T(4,128)(2,1)} %slice.332), channel_id=1, source_target_pairs={{0,1},{1,2},{2,3},{3,4},{4,5},{5,6},{6,7},{7,8},{8,9},{9,10},{10,1... | collective-permute-start | bytes 2312 | tf_op jit(solution)/shard_map/ppermute | solution.py:28
  53.0 0.6 slice.333
  53.6 1.6 %convolution_bitcast_fusion = f32[8,8]{1,0:T(8,128)} fusion(f32[8,32,3,128]{3,1,2,0:T(8,128)S(1)} %copy-done.5), kind=kOutput, calls=%fused_computation.20 | convolution fusion | flops 9437184 | bytes 393472 | tf_op jit(solution)/shard_map/mbcj,nbcj->mn/dot_general | solution.py:191
  55.3 1.3 %reshape.810 = f32[64]{0:T(128)} reshape(f32[8,8]{1,0:T(8,128)} %convolution_bitcast_fusion) | data formatting | bytes 512 | tf_op jit(solution)/shard_map/reshape | solution.py:193
  56.6 2.0 %fusion.107 = f32[32,3,128]{2,1,0:T(4,128)} fusion(bf16[32,3,128]{2,1,0:T(4,128)(2,1)} %copy-done.8, bf16[32,128,128]{2,1,0:T(8,128)(2,1)S(1)} %copy-done.6), kind=kOutput, calls=%fused_computation.214 | convolution fusion | flops 3145728 | bytes 1122304 | tf_op jit(solution)/shard_map/bcj,bij->bci/dot_general | solution.py:181
  58.6 0.5 broadcast.290
  59.2 0.7 reduce.21
  60.0 1.0 %reshape.809 = f32[128,384]{1,0:T(8,128)S(1)} reshape(f32[32,4,384]{2,1,0:T(4,128)} %all-to-all-done.1) | data formatting | bytes 393216 | tf_op jit(solution)/shard_map/reshape | solution.py:169
  61.1 0.2 fusion.85
  61.4 1.9 %fusion.1 = f32[32,3,128]{2,1,0:T(4,128)S(1)} fusion(f32[32,3,128]{2,1,0:T(4,128)} %fusion.107, bf16[32,128,128]{2,1,0:T(8,128)(2,1)} %param.24, f32[32,3,128]{2,0,1:T(8,128)S(1)} %fusion.85, f32[32,3,128]{2,0,1:T(8,128)} %param.25, bf16[31,3,128]{2,1,0:T(4,128)(2,1)} %slice.333, bf16[1,3,128]{2,1,0:T(4,128)(2,1)} %collective-permute-done.2), kind=kOutput, calls=%fused_computation.19 | convolution fusion | flops 3244032 | bytes 1269760 | tf_op jit(solution)/shard_map/bcj,bij->bci/dot_general | solution.py:184
  63.3 1.1 %convolution_bitcast_fusion.3 = f32[8]{0:T(128)S(1)} fusion(f32[8,32,3,128]{3,1,2,0:T(8,128)S(1)} %copy-done.5, f32[32,3,128,1]{2,1,0,3:T(4,128)S(1)} %bitcast.225), kind=kOutput, calls=%fused_computation.25 | convolution fusion | flops 1179648 | bytes 442400 | tf_op jit(solution)/shard_map/mbcj,bcj->m/dot_general | solution.py:188
  64.5 12.3 %all_to_all.25 = f32[32,1,72]{2,1,0:T(1,128)S(1)} all-to-all(f32[32,1,72]{2,1,0:T(1,128)S(1)} %broadcast_in_dim.15), channel_id=1, replica_groups=mesh['group'=4,'dev'=8] {'group','dev'}, dimensions={0} | all-to-all | bytes 18432 | tf_op jit(solution)/shard_map/all_to_all | solution.py:194
  77.0 0.7 cholesky.16
  77.8 0.6 compare_reduce_fusion
  78.4 0.6 fusion.88
  79.1 0.6 custom-call.8
  79.7 0.2 convolution_bitcast_fusion.2
  80.0 0.7 fusion.14
  80.8 0.2 convolution_convert_fusion
  81.0 0.7 reshape.813
  81.7 2.6 %all-to-all-start.3 = ((bf16[32,4,384]{2,1,0:T(4,128)(2,1)}), bf16[32,4,384]{2,1,0:T(4,128)(2,1)S(1)}, u32[]{:S(2)}, u32[]{:S(2)}) async-start(bf16[32,4,384]{2,1,0:T(4,128)(2,1)} %reshape.813), calls=%async_computation.3 | async-start | bytes 196608 | tf_op jit(solution)/shard_map/all_to_all | solution.py:214
  84.3 0.6 copy.79
  84.9 7.1 %all-to-all-done.3 = bf16[32,4,384]{2,1,0:T(4,128)(2,1)S(1)} async-done(((bf16[32,4,384]{2,1,0:T(4,128)(2,1)}), bf16[32,4,384]{2,1,0:T(4,128)(2,1)S(1)}, u32[]{:S(2)}, u32[]{:S(2)}) %all-to-all-start.3) | async-done | bytes 98336 | tf_op jit(solution)/shard_map/all_to_all | solution.py:214
  92.0 0.7 gather_fusion
  92.8 1.2 %fusion.108 = f32[64,3,128]{2,1,0:T(4,128)S(1)} fusion(bf16[64,3,128]{2,1,0:T(4,128)(2,1)S(1)} %reshape.815, bf16[64,128,128]{2,1,0:T(8,128)(2,1)S(1)} %copy-done), kind=kOutput, calls=%fused_computation.215 | convolution fusion | flops 6291456 | bytes 2244608 | tf_op jit(solution)/shard_map/bij,bcj->bci/dot_general | solution.py:222
  93.9 0.7 copy.80
  (87 shorter events, 2.6 us)
Async XLA Ops:
  0.6 39.9 %copy-start = (bf16[64,128,128]{2,1,0:T(8,128)(2,1)S(1)}, bf16[64,128,128]{2,1,0:T(8,128)(2,1)}, u32[]{:S(2)}) copy-start(bf16[64,128,128]{2,1,0:T(8,128)(2,1)} %param.18) | copy-start | bytes 6291460
  0.6 1.4 %copy-start.1 = (f32[1,320,128]{2,1,0:T(8,128)S(1)}, f32[1,320,128]{2,1,0:T(8,128)}, u32[]{:S(2)}) copy-start(f32[1,320,128]{2,1,0:T(8,128)} %param.15) | copy-start | bytes 491524
  0.7 2.8 %copy-start.10 = (f32[1,320,128]{2,1,0:T(8,128)S(1)}, f32[1,320,128]{2,1,0:T(8,128)}, u32[]{:S(2)}) copy-start(f32[1,320,128]{2,1,0:T(8,128)} %param.17) | copy-start | bytes 491524
  2.0 3.1 %copy-start.3 = (f32[320,128]{1,0:T(8,128)}, f32[320,128]{1,0:T(8,128)S(1)}, u32[]{:S(2)}) copy-start(f32[320,128]{1,0:T(8,128)S(1)} %get-tuple-element.33) | copy-start | bytes 491524
  2.7 8.8 %copy-start.12 = (s32[64,1]{0,1:T(1,128)S(1)}, s32[64,1]{0,1:T(1,128)}, u32[]{:S(2)}) copy-start(s32[64,1]{0,1:T(1,128)} %param.21) | copy-start | bytes 772
  3.4 8.4 %copy-start.17 = (s32[64]{0:T(128)S(1)}, s32[64]{0:T(128)}, u32[]{:S(2)}) copy-start(s32[64]{0:T(128)} %param.22) | copy-start | bytes 772
  4.2 16.9 %copy-start.16 = (f32[5]{0:T(128)S(1)}, f32[5]{0:T(128)}, u32[]{:S(2)}) copy-start(f32[5]{0:T(128)} %constant.89.clone) | copy-start | bytes 64
  5.1 24.1 %collective-permute-start.1 = (f32[5,1,320,128]{3,2,1,0:T(8,128)}, f32[5,1,320,128]{3,2,1,0:T(8,128)}, u32[]{:S(2)}, u32[]{:S(2)}) collective-permute-start(f32[5,1,320,128]{3,2,1,0:T(8,128)} %pad_maximum_fusion.3), channel_id=1, source_target_pairs={{1,0},{2,1},{3,2},{4,3},{5,4},{6,5},{7,6},{8,7},{9,8},{10,9},{11,1... | collective-permute-start | bytes 2457608 | tf_op jit(solution)/shard_map/ppermute | solution.py:20
  11.5 20.1 %collective-permute-start = (f32[5,1,320,128]{3,2,1,0:T(8,128)}, f32[5,1,320,128]{3,2,1,0:T(8,128)}, u32[]{:S(2)}, u32[]{:S(2)}) collective-permute-start(f32[5,1,320,128]{3,2,1,0:T(8,128)} %pad_maximum_fusion.3), channel_id=1, source_target_pairs={{0,1},{1,2},{2,3},{3,4},{4,5},{5,6},{6,7},{7,8},{8,9},{9,10},{10,1... | collective-permute-start | bytes 2457608 | tf_op jit(solution)/shard_map/ppermute | solution.py:19
  11.9 10.9 %copy-start.13 = (s32[64]{0:T(128)}, s32[64]{0:T(128)S(1)}, u32[]{:S(2)}) copy-start(s32[64]{0:T(128)S(1)} %fusion.92) | copy-start | bytes 772
  13.4 31.9 %all-to-all-start = ((f32[32,1,4]{2,1,0:T(1,128)}), f32[32,1,4]{2,1,0:T(1,128)S(1)}, u32[]{:S(2)}, u32[]{:S(2)}) async-start(f32[32,1,4]{2,1,0:T(1,128)} %bitcast.30), calls=%async_computation | async-start | bytes 32768 | tf_op jit(solution)/shard_map/all_to_all | solution.py:161
  25.1 0.9 copy-start.4
  36.2 3.5 %copy-start.11 = (f32[64,3,128]{2,0,1:T(8,128)S(1)}, f32[64,3,128]{2,0,1:T(8,128)}, u32[]{:S(2)}) copy-start(f32[64,3,128]{2,0,1:T(8,128)} %param.20) | copy-start | bytes 294916
  36.6 0.9 copy-start.2
  40.6 13.1 %copy-start.5 = (f32[8,32,3,128]{3,1,2,0:T(8,128)S(1)}, f32[8,32,3,128]{3,1,2,0:T(8,128)}, u32[]{:S(2)}) copy-start(f32[8,32,3,128]{3,1,2,0:T(8,128)} %param.27) | copy-start | bytes 1179652
  40.6 16.0 %copy-start.6 = (bf16[32,128,128]{2,1,0:T(8,128)(2,1)S(1)}, bf16[32,128,128]{2,1,0:T(8,128)(2,1)}, u32[]{:S(2)}) copy-start(bf16[32,128,128]{2,1,0:T(8,128)(2,1)} %param.23) | copy-start | bytes 3145732
  45.4 14.6 %all-to-all-start.1 = ((f32[32,4,384]{2,1,0:T(4,128)}), f32[32,4,384]{2,1,0:T(4,128)}, u32[]{:S(2)}, u32[]{:S(2)}) async-start(f32[32,4,384]{2,1,0:T(4,128)} %reshape.808), calls=%async_computation.1 | async-start | bytes 393216 | tf_op jit(solution)/shard_map/all_to_all | solution.py:154
  49.7 3.3 %copy-start.8 = (bf16[32,3,128]{2,1,0:T(4,128)(2,1)}, bf16[32,3,128]{2,1,0:T(4,128)(2,1)S(1)}, u32[]{:S(2)}) copy-start(bf16[32,3,128]{2,1,0:T(4,128)(2,1)S(1)} %copy.116) | copy-start | bytes 73732
  50.4 11.0 %collective-permute-start.2 = (bf16[1,3,128]{2,1,0:T(4,128)(2,1)}, bf16[1,3,128]{2,1,0:T(4,128)(2,1)}, u32[]{:S(2)}, u32[]{:S(2)}) collective-permute-start(bf16[1,3,128]{2,1,0:T(4,128)(2,1)} %slice.332), channel_id=1, source_target_pairs={{0,1},{1,2},{2,3},{3,4},{4,5},{5,6},{6,7},{7,8},{8,9},{9,10},{10,1... | collective-permute-start | bytes 2312 | tf_op jit(solution)/shard_map/ppermute | solution.py:28
  58.6 5.8 %copy-start.15 = (f32[64]{0:T(128)S(1)}, f32[64]{0:T(128)}, u32[]{:S(2)}) copy-start(f32[64]{0:T(128)} %reshape.810) | copy-start | bytes 772
  58.6 21.4 %copy-start.7 = (f32[8,32,3,128]{3,1,2,0:T(8,128)S(1)}, f32[8,32,3,128]{3,1,2,0:T(8,128)}, u32[]{:S(2)}) copy-start(f32[8,32,3,128]{3,1,2,0:T(8,128)} %param.28) | copy-start | bytes 1179652
  60.0 20.7 %copy-start.9 = (f32[32,3,128]{2,0,1:T(8,128)S(1)}, f32[32,3,128]{2,0,1:T(8,128)}, u32[]{:S(2)}) copy-start(f32[32,3,128]{2,0,1:T(8,128)} %param.26) | copy-start | bytes 147460
  61.1 23.1 %copy-start.14 = (s32[64]{0:T(128)S(1)}, s32[64]{0:T(128)}, u32[]{:S(2)}) copy-start(s32[64]{0:T(128)} %copy-done.13) | copy-start | bytes 772
  81.7 10.3 %all-to-all-start.3 = ((bf16[32,4,384]{2,1,0:T(4,128)(2,1)}), bf16[32,4,384]{2,1,0:T(4,128)(2,1)S(1)}, u32[]{:S(2)}, u32[]{:S(2)}) async-start(bf16[32,4,384]{2,1,0:T(4,128)(2,1)} %reshape.813), calls=%async_computation.3 | async-start | bytes 196608 | tf_op jit(solution)/shard_map/all_to_all | solution.py:214

commit v2 on v0

v2 whole, which is shorter than its diff:
```python
import functools

import jax
import jax.numpy as jnp
from jax import lax
from jax.experimental import pallas as pl
from jax.experimental.pallas import tpu as pltpu
from jax.sharding import PartitionSpec as P

ratio_heat = 1.4
step_ratio = 0.03
AXES = ("group", "dev")
MESH = pl.DeviceIdType.MESH
LAST = (((1,), (1,)), ((), ()))


def conserve(prim):
    dens, u, v, w, press = prim
    energy = press / (ratio_heat - 1.0) + 0.5 * dens * (u * u + v * v + w * w)
    return (dens, dens * u, dens * v, dens * w, energy)


def flux_parts(prim, axis):
    state = conserve(prim)
    normal = prim[1 + axis]
    press = prim[4]
    rows = [row * normal for row in state]
    rows[1 + axis] = rows[1 + axis] + press
    rows[4] = rows[4] + press * normal
    speed = jnp.abs(normal) + jnp.sqrt(ratio_heat * press / prim[0])
    return state, rows, speed


def face_difference(low, mid, high, axis):
    state_l, flux_l, speed_l = flux_parts(low, axis)
    state_m, _, speed_m = flux_parts(mid, axis)
    state_h, flux_h, speed_h = flux_parts(high, axis)
    upper = jnp.maximum(speed_m, speed_h)
    lower = jnp.maximum(speed_l, speed_m)
    return [
        0.5 * (fh - fl) - 0.5 * (upper * (sh - sm) - lower * (sm - sl))
        for fh, fl, sh, sm, sl in zip(flux_h, flux_l, state_h, state_m, state_l)
    ]


def advance(mid, x_pair, y_pair, z_pair):
    div_x = face_difference(x_pair[0], mid, x_pair[1], 0)
    div_y = face_difference(y_pair[0], mid, y_pair[1], 1)
    div_z = face_difference(z_pair[0], mid, z_pair[1], 2)
    return [
        row - step_ratio * (a + b + c)
        for row, a, b, c in zip(conserve(mid), div_x, div_y, div_z)
    ]


def flow_kernel(dens_ref, vel_ref, press_ref, low_ref, high_ref, out_ref):
    height, lanes = dens_ref.shape[1:]
    chunk = next(c for c in (32, 16, 8, height) if height % c == 0)
    row = lax.broadcasted_iota(jnp.int32, (chunk, lanes), 0)
    lane = lax.broadcasted_iota(jnp.int32, (chunk, lanes), 1)
    fields = [dens_ref.at[0]] + [vel_ref.at[i, 0] for i in range(3)] + [press_ref.at[0]]
    for start in range(0, height, chunk):
        rows = slice(start, start + chunk)
        before = (start - 1) % height
        after = (start + chunk) % height
        mid = [f[rows, :] for f in fields]
        y_low = [
            jnp.where(row == 0, f[before : before + 1, :], pltpu.roll(m, 1, 0))
            for f, m in zip(fields, mid)
        ]
        y_high = [
            jnp.where(row == chunk - 1, f[after : after + 1, :], pltpu.roll(m, chunk - 1, 0))
            for f, m in zip(fields, mid)
        ]
        signs = (1.0, 1.0, 1.0, -1.0, 1.0)
        z_low = [jnp.where(lane == 0, s * m, pltpu.roll(m, 1, 1)) for s, m in zip(signs, mid)]
        z_high = [jnp.where(lane == lanes - 1, m, pltpu.roll(m, lanes - 1, 1)) for m in mid]
        x_low = [low_ref[i, rows, :].astype(jnp.float32) for i in range(5)]
        x_high = [high_ref[i, rows, :].astype(jnp.float32) for i in range(5)]
        result = advance(mid, (x_low, x_high), (y_low, y_high), (z_low, z_high))
        for i in range(5):
            out_ref[i, 0, rows, :] = result[i]


def thirds(value):
    high = value.astype(jnp.bfloat16)
    rest = value - high.astype(jnp.float32)
    middle = rest.astype(jnp.bfloat16)
    low = (rest - middle.astype(jnp.float32)).astype(jnp.bfloat16)
    return high, middle, low


def select_rows(chooser, value):
    parts = [
        jnp.dot(chooser, part, preferred_element_type=jnp.float32) for part in thirds(value)
    ]
    return (parts[2] + parts[1]) + parts[0]


def couple_kernel(
    peers,
    width,
    wall_ref,
    prim_ref,
    normals_ref,
    index_ref,
    rbf_ref,
    pick_ref,
    place_ref,
    tags_ref,
    stiff_ref,
    coup_ref,
    inv_ref,
    disp_ref,
    res_ref,
    dif_ref,
    low_ref,
    high_ref,
    next_ref,
    motion_ref,
    side_ref,
    prior_ref,
    tag_in,
    load_out,
    load_in,
    reply_out,
    reply_in,
    stat_out,
    stat_in,
    loads,
    slots,
    solid,
    products,
    near_send,
    near_recv,
    tag_send,
    tag_recv,
    load_send,
    load_recv,
    stat_send,
    stat_recv,
    reply_send,
    reply_recv,
):
    me = lax.axis_index("group") * width + lax.axis_index("dev")
    blocks = index_ref.shape[0]
    count = disp_ref.shape[0]
    columns = res_ref.shape[0]
    capacity = tags_ref.shape[1]
    nodes = index_ref.shape[1]

    def place(peer):
        return (peer // width, peer % width)

    def hop(distance):
        return (me + distance) % peers

    barrier = pltpu.get_barrier_semaphore()

    def greet(step, carry):
        pl.semaphore_signal(barrier, inc=1, device_id=place(hop(step)), device_id_type=MESH)
        return carry

    lax.fori_loop(1, peers, greet, 0)
    pl.semaphore_wait(barrier, peers - 1)

    def near(slot, src, dst, distance):
        return pltpu.make_async_remote_copy(
            src_ref=src,
            dst_ref=dst,
            send_sem=near_send.at[slot],
            recv_sem=near_recv.at[slot],
            device_id=place(hop(distance)),
            device_id_type=MESH,
        )

    wall_up = near(0, wall_ref.at[0], side_ref.at[0], 1)
    wall_down = near(1, wall_ref.at[0], side_ref.at[1], peers - 1)
    prior = near(2, disp_ref.at[count - 1], prior_ref, 1)
    bulk_up = near(3, prim_ref, low_ref, 1)
    bulk_down = near(4, prim_ref, high_ref, peers - 1)

    def spread(src, dst, send, recv, indexed):
        def begin(step, carry):
            peer = hop(step)
            pltpu.make_async_remote_copy(
                src_ref=src.at[peer] if indexed else src,
                dst_ref=dst.at[me],
                send_sem=send.at[step],
                recv_sem=recv.at[step],
                device_id=place(peer),
                device_id_type=MESH,
            ).start()
            return carry

        lax.fori_loop(1, peers, begin, 0)

    def gather(src, dst, send, recv, indexed):
        def finish(step, carry):
            pltpu.make_async_remote_copy(
                src_ref=src.at[hop(step)] if indexed else src,
                dst_ref=dst.at[hop(peers - step)],
                send_sem=send.at[step],
                recv_sem=recv.at[step],
                device_id=place(hop(step)),
                device_id_type=MESH,
            ).wait()
            return carry

        lax.fori_loop(1, peers, finish, 0)

    wall_up.start()
    wall_down.start()
    prior.start()
    spread(tags_ref, tag_in, tag_send, tag_recv, True)
    bulk_up.start()
    bulk_down.start()
    tag_in[me] = tags_ref[me]

    products[...] = jnp.zeros_like(products)
    for m in range(columns):
        for n in range(m, columns):
            line = jnp.sum(jnp.sum(res_ref[m] * res_ref[n], axis=0), axis=0, keepdims=True)
            products[m * columns + n : m * columns + n + 1, :] = line
            products[n * columns + m : n * columns + m + 1, :] = line

    wall_up.wait()
    wall_down.wait()

    def variant(i):
        return [wall_ref[i, k : k + 1, :] for k in range(5)]

    mid = variant(0)
    mirror = list(mid)
    mirror[3] = -mirror[3]
    beside = [[side_ref[j, k : k + 1, :] for k in range(5)] for j in range(2)]
    bottom = advance(mid, beside, (variant(3), variant(2)), (mirror, variant(1)))
    kinetic = bottom[1] * bottom[1] + bottom[2] * bottom[2] + bottom[3] * bottom[3]
    wall = (ratio_heat - 1.0) * (bottom[4] - 0.5 * kinetic / bottom[0])

    index = index_ref[...]
    low = index % nodes
    found = jnp.zeros(index.shape, jnp.float32)
    for part in range(wall.shape[1] // nodes):
        source = jnp.broadcast_to(wall[:, part * nodes : (part + 1) * nodes], index.shape)
        taken = jnp.take_along_axis(source, low, axis=1)
        found = jnp.where(index // nodes == part, taken, found)
    slots[0:blocks, 0:nodes] = found
    for b in range(blocks):
        weighted = (slots[b : b + 1, 0:nodes] * normals_ref[b]).astype(jnp.bfloat16)
        loads[b, 0:3, :] = jnp.dot(weighted, rbf_ref[b], preferred_element_type=jnp.float32)
    spans = [slice(c * nodes, (c + 1) * nodes) for c in range(3)]
    for c in range(3):
        slots[:, spans[c]] = select_rows(place_ref[...], loads[:, c, :])
    for p in range(peers):
        load_out[p] = slots[p * capacity : (p + 1) * capacity, :]
    spread(load_out, load_in, load_send, load_recv, True)
    load_in[me] = load_out[me]

    prior.wait()
    first = (me > 0).astype(jnp.float32)
    for t in range(count):
        half = disp_ref[t].astype(jnp.bfloat16)
        earlier = disp_ref[t - 1] if t else prior_ref[...] * first
        part = lax.dot_general(half, stiff_ref[t], LAST, preferred_element_type=jnp.float32)
        part = part + lax.dot_general(
            earlier.astype(jnp.bfloat16), coup_ref[t], LAST, preferred_element_type=jnp.float32
        )
        solid[t, 0:3, :] = part

    gather(tags_ref, tag_in, tag_send, tag_recv, True)
    for p in range(peers):
        slots[p * capacity : (p + 1) * capacity, spans[0]] = tag_in[p]
    tags = slots[:, spans[0]]
    lane = lax.broadcasted_iota(jnp.int32, tags.shape, 1).astype(jnp.float32)
    chooser = (tags == lane).astype(jnp.float32)[:, 0:count].astype(jnp.bfloat16)
    turned = tags.T[0:count, :]
    line_id = lax.broadcasted_iota(jnp.int32, turned.shape, 0).astype(jnp.float32)
    collector = (turned == line_id).astype(jnp.float32).astype(jnp.bfloat16)

    gather(load_out, load_in, load_send, load_recv, True)
    for p in range(peers):
        slots[p * capacity : (p + 1) * capacity, :] = load_in[p]
    for c in range(3):
        solid[:, c, :] = solid[:, c, :] - select_rows(collector, slots[:, spans[c]])
    change = -inv_ref[...] * solid[:, 0:3, :]
    for m in range(columns):
        line = jnp.sum(jnp.sum(res_ref[m] * change, axis=0), axis=0, keepdims=True)
        at = columns * columns + m
        products[at : at + 1, :] = line
    stat_out[...] = jnp.sum(products[...].T, axis=0, keepdims=True)
    spread(stat_out, stat_in, stat_send, stat_recv, False)
    stat_in[me] = stat_out[...]
    solid[:, 0:3, :] = disp_ref[...] + change
    gather(stat_out, stat_in, stat_send, stat_recv, False)
    total = jnp.sum(stat_in[...], axis=0)
    shape = (columns, nodes)
    m_id = lax.broadcasted_iota(jnp.int32, shape, 0)
    n_id = lax.broadcasted_iota(jnp.int32, shape, 1)
    source = jnp.where(
        n_id < columns, m_id * columns + n_id, columns * columns + m_id
    )
    matrix = jnp.take_along_axis(jnp.broadcast_to(total, shape), source, axis=1)
    for k in range(columns):
        line = matrix[k : k + 1, :]
        scaled = line / matrix[k : k + 1, k : k + 1]
        matrix = jnp.where(m_id == k, scaled, matrix - matrix[:, k : k + 1] * scaled)
    mixing = -matrix[:, columns : columns + 1]
    result = solid[:, 0:3, :]
    for m in range(columns):
        result = result + dif_ref[m] * mixing[m : m + 1, :].reshape(1, 1, 1)
    next_ref[...] = result
    solid[:, 0:3, :] = result
    for c in range(3):
        rows = solid[:, c, :].astype(jnp.bfloat16)
        slots[:, spans[c]] = jnp.dot(chooser, rows, preferred_element_type=jnp.float32)
    for p in range(peers):
        reply_out[p] = slots[p * capacity : (p + 1) * capacity, :].astype(jnp.bfloat16)
    spread(reply_out, reply_in, reply_send, reply_recv, True)
    reply_in[me] = reply_out[me]
    gather(reply_out, reply_in, reply_send, reply_recv, True)
    for p in range(peers):
        slots[p * capacity : (p + 1) * capacity, :] = reply_in[p].astype(jnp.float32)
    for c in range(3):
        rows = slots[:, spans[c]].astype(jnp.bfloat16)
        loads[:, c, :] = jnp.dot(pick_ref[...], rows, preferred_element_type=jnp.float32)
    for b in range(blocks):
        reply = loads[b, 0:3, :].astype(jnp.bfloat16)
        motion_ref[b] = lax.dot_general(
            reply, rbf_ref[b], LAST, preferred_element_type=jnp.float32
        )
    bulk_up.wait()
    bulk_down.wait()


def on_device(
    density,
    velocity,
    pressure,
    rbf_blocks,
    correlation,
    normals,
    routes,
    targets,
    stiffness,
    coupling,
    inverse_diag,
    displacement,
    diff_res,
    diff_disp,
):
    f32, bf16 = jnp.float32, jnp.bfloat16
    width = lax.axis_size("dev")
    peers = lax.axis_size(AXES)
    blocks, nodes = correlation.shape
    count = displacement.shape[0]
    columns = diff_res.shape[0]
    height, depth = density.shape[1:]
    capacity = max(2, 2 * blocks // peers)
    slot_count = peers * capacity

    ends = jnp.concatenate([density[None], velocity, pressure[None]], axis=0)[:, 0, :, 0:2]
    ends = jnp.transpose(ends, (2, 0, 1))
    ends = jnp.stack(
        [ends[0], ends[1], jnp.roll(ends[0], -1, axis=1), jnp.roll(ends[0], 1, axis=1)]
    )
    padded = -(-height // nodes) * nodes
    ends = jnp.pad(ends, ((0, 0), (0, 3), (0, padded - height)), constant_values=1.0)
    prim = jnp.concatenate([density, velocity[:, 0], pressure], axis=0).astype(bf16)

    owner = routes[:, 0]
    same = (owner[:, None] == owner[None, :]) & (
        jnp.arange(blocks)[:, None] > jnp.arange(blocks)[None, :]
    )
    slot_id = owner * capacity + jnp.sum(same.astype(jnp.int32), axis=1)
    chosen = slot_id[:, None] == jnp.arange(slot_count, dtype=jnp.int32)[None, :]
    pick = chosen.astype(bf16)
    put = (jnp.arange(slot_count, dtype=jnp.int32)[:, None] == slot_id[None, :])
    tag = jnp.sum(jnp.where(chosen, targets[:, None] + 1, 0), axis=0) - 1
    tags = jnp.broadcast_to(
        tag.astype(f32).reshape(peers, capacity)[:, :, None], (peers, capacity, nodes)
    )

    vmem = pl.BlockSpec(memory_space=pltpu.VMEM)
    anywhere = pl.BlockSpec(memory_space=pl.ANY)
    dma = pltpu.SemaphoreType.DMA
    halo = jax.ShapeDtypeStruct((5, height, depth), bf16)
    width_row = 3 * nodes
    low, high, disp_next, wall_motion = pl.pallas_call(
        functools.partial(couple_kernel, peers, width),
        out_shape=(
            halo,
            halo,
            jax.ShapeDtypeStruct(displacement.shape, f32),
            jax.ShapeDtypeStruct(normals.shape, f32),
        ),
        in_specs=[vmem, anywhere] + [vmem] * 12,
        out_specs=(anywhere, anywhere, vmem, vmem),
        scratch_shapes=[
            pltpu.VMEM((2, 8, padded), f32),
            pltpu.VMEM((3, nodes), f32),
            pltpu.VMEM((peers, capacity, nodes), f32),
            pltpu.VMEM((peers, capacity, width_row), f32),
            pltpu.VMEM((peers, capacity, width_row), f32),
            pltpu.VMEM((peers, capacity, width_row), bf16),
            pltpu.VMEM((peers, capacity, width_row), bf16),
            pltpu.VMEM((1, nodes), f32),
            pltpu.VMEM((peers, 1, nodes), f32),
            pltpu.VMEM((blocks, 8, nodes), f32),
            pltpu.VMEM((slot_count, width_row), f32),
            pltpu.VMEM((count, 8, nodes), f32),
            pltpu.VMEM((nodes, nodes), f32),
            dma((5,)),
            dma((5,)),
        ]
        + [dma((peers,))] * 8,
        compiler_params=pltpu.CompilerParams(collective_id=0, has_side_effects=True),
    )(
        ends,
        prim,
        normals,
        correlation,
        rbf_blocks,
        pick,
        put.astype(bf16),
        tags,
        stiffness,
        coupling,
        inverse_diag,
        displacement,
        diff_res,
        diff_disp,
    )
    fluid_next = pl.pallas_call(
        flow_kernel,
        out_shape=jax.ShapeDtypeStruct((5,) + density.shape, f32),
        in_specs=[vmem] * 5,
        out_specs=vmem,
    )(density, velocity, pressure, low, high)
    return (fluid_next, disp_next, wall_motion)


def solution(mesh):
    placed = (
        P(("group", "dev"), None, None),
        P(None, ("group", "dev"), None, None),
        P(("group", "dev"), None, None),
        P(("group", "dev"), None, None),
        P(("group", "dev"), None),
        P(("group", "dev"), None, None),
        P(("group", "dev"), None),
        P(("group", "dev")),
        P(("group", "dev"), None, None),
        P(("group", "dev"), None, None),
        P(("group", "dev"), None, None),
        P(("group", "dev"), None, None),
        P(None, ("group", "dev"), None, None),
        P(None, ("group", "dev"), None, None),
    )
    return jax.shard_map(
        on_device,
        mesh=mesh,
        in_specs=placed,
        out_specs=(
            P(None, ("group", "dev"), None, None),
            P(("group", "dev"), None, None),
            P(("group", "dev"), None, None),
        ),
        check_vma=False,
    )
```

time: 172 us -> 60.2 us (0.35)
  local copies, waits for them, and re-layouts: 66.3 us -> 10.1 us
  Pallas kernels: 0 us -> 45.9 us
  blocking collectives: 40 us -> 0 us
  starting transfers between devices: 23.6 us -> 0 us
  other arithmetic: 20.4 us -> 3.17 us
  matrix products: 9.77 us -> 0 us
  waiting for transfers between devices: 9.52 us -> 0 us
    gather x2 -> x0, local copies, waits for them, and re-layouts: 51.9 us -> none  [the longest x1 51.2 us: on_device(): wall_row[correlation][:, None, :] * normals]
    pallas_call x0 -> x2, Pallas kernels: none -> 45.9 us  [the longest x1 41.3 us: on_device(): pl.pallas_call(functools.partial(couple_kernel, peers, width), out_shape=...]
    psum x1 -> x0, blocking collectives: 40 us -> none  [on_device(): lax.psum((gram_local, projected_local), ('group', 'dev'))]
    all_to_all x3 -> x0, starting transfers between devices: 14.5 us -> none  [the longest x1 5.7 us: on_device(): lax.all_to_all(send_tag.reshape(peer_count, capacity), ('group', 'dev'),...]
    dot_general x9 -> x0, matrix products: 9.5 us -> none  [the longest x1 1.94 us: on_device(): jnp.einsum('bcj,bij->bci', earlier, coupling, preferred_element_type=jnp....]
    ppermute x3 -> x0, starting transfers between devices: 9.07 us -> none  [the longest x1 6.4 us: extended(): after = lax.ppermute(leading, axis, down)]
    all_to_all x3 -> x0, waiting for transfers between devices: 7.11 us -> none  [the longest x1 7.1 us: on_device(): lax.all_to_all(replies.reshape(peer_count, capacity, width_row), ('group'...]
    unnamed x39 -> x34, local copies, waits for them, and re-layouts: 3.53 us -> 9.11 us
  transfers between devices with their start and end apart: 6 -> 0, of which waited for: 2 -> 0; matrix products, arithmetic and copies ran while one was open for 47% -> 0% of each run, Pallas kernels for 0% -> 0%
where the time goes in v2:
time: 60.2 us; the launch traced here: 60 us
  Pallas kernels  45.9 us (76%)
  local copies, waits for them, and re-layouts  10.1 us (17%)
  other arithmetic  3.17 us (5%)
  between operations  0.83 us (1%)
    pallas_call x1, Pallas kernels, on_device(): pl.pallas_call(functools.partial(couple_kernel, peers, width), out_shape=...  41.3 us
    unnamed x34, local copies, waits for them, and re-layouts  9.11 us
    pallas_call x1, Pallas kernels, on_device(): pl.pallas_call(flow_kernel, out_shape=jax.ShapeDtypeStruct((5,) + density...  4.63 us

profile of v2, /device:TPU:0, one launch (start us, length us, event | category | flops | bytes accessed | tf_op | source)
XLA Modules:
  0.0 60.0 jit_solution(16490996817057693764)
XLA Ops:
  0.6 0.0 copy-start
  0.6 0.0 copy-start.1
  0.7 0.0 copy-start.2
  0.7 0.0 copy-start.11
  0.7 0.0 copy-start.10
  0.7 1.4 %copy.41 = f32[3,1,320,128]{2,0,3,1:T(4,128)S(1)} copy(f32[3,1,320,128]{3,2,1,0:T(8,128)} %vel_ref.1) | data formatting | bytes 983040 | tf_op args[1]
  2.1 1.1 %copy.39 = f32[1,320,128]{1,0,2:T(1,128)S(1)} copy(f32[1,320,128]{2,1,0:T(8,128)} %dens_ref.1) | data formatting | bytes 327680 | tf_op args[0]
  3.2 0.0 copy-start.3
  3.2 1.1 %copy.40 = f32[1,320,128]{1,0,2:T(1,128)S(1)} copy(f32[1,320,128]{2,1,0:T(8,128)} %press_ref.1) | data formatting | bytes 327680 | tf_op args[2]
  4.3 0.0 copy-start.4
  4.4 0.1 fusion.6
  4.5 0.1 fusion.7
  4.5 0.0 copy-start.6
  4.5 0.1 maximum_bitcast_fusion
  4.6 0.6 %select_maximum_fusion.wall_ref = f32[4,8,384]{2,1,0:T(8,128)} fusion(f32[1,5,320]{2,1,0:T(8,128)S(1)} %get-tuple-element.25, f32[1,5,320]{2,1,0:T(8,128)S(1)} %get-tuple-element.24, f32[2,5,320]{2,1,0:T(8,128)S(1)} %fusion.4), kind=kLoop, calls=%fused_computation.5 | loop fusion | flops 135168 | bytes 74752 | tf_op jit(solution)/shard_map/stack | solution.py:364
  5.2 0.0 copy-done.11
  5.3 0.2 convert_reduce_fusion
  5.4 0.0 copy-done.10
  5.5 0.1 select_reduce_fusion
  5.6 0.1 convert_element_type.24
  5.7 0.7 %broadcast_in_dim.34.tags_ref = f32[32,4,128]{2,1,0:T(4,128)} broadcast(f32[32,4]{1,0:T(8,128)S(1)} %convert_element_type.24), dimensions={0,1} | broadcast | bytes 66048 | tf_op jit(solution)/shard_map/broadcast_in_dim | solution.py:380
  6.4 0.0 copy-start.8
  6.4 0.7 %fusion.2.pick_ref = bf16[64,128]{1,0:T(8,128)(2,1)} fusion(s32[64]{0:T(128)S(1)} %fusion.5), kind=kLoop, calls=%fused_computation.11 | loop fusion | flops 16384 | bytes 16640 | tf_op jit(solution)/shard_map/convert_element_type | solution.py:377
  7.1 0.6 %fusion.1.place_ref = bf16[128,64]{1,0:T(8,128)(2,1)} fusion(s32[64]{0:T(128)S(1)} %multiply_add_fusion), kind=kLoop, calls=%fused_computation.4 | loop fusion | flops 16384 | bytes 16640 | tf_op jit(solution)/shard_map/convert_element_type | solution.py:425
  7.7 0.0 copy-done
  7.7 0.0 copy-start.9
  7.8 0.0 copy-done.1
  7.8 0.0 copy-done.2
  7.8 0.8 %pad_maximum_fusion.prim_ref = bf16[5,320,128]{2,1,0:T(8,128)(2,1)} fusion(bf16[1,320,128]{2,1,0:T(8,128)(2,1)S(1)} %convert.12, bf16[3,320,128]{2,1,0:T(8,128)(2,1)S(1)} %fusion, bf16[1,320,128]{2,1,0:T(8,128)(2,1)S(1)} %convert.10), kind=kLoop, calls=%fused_computation.1 | loop fusion | flops 409600 | bytes 819200 | tf_op jit(solution)/shard_map/concatenate | solution.py:369
  8.6 0.0 copy-done.3
  8.6 1.1 %copy.46.res_ref = f32[8,32,3,128]{3,2,1,0:T(4,128)} copy(f32[8,32,3,128]{3,1,2,0:T(8,128)S(1)} %copy-done.3) | data formatting | bytes 786432 | tf_op args[12]
  9.7 0.0 copy-done.4
  9.7 1.1 %copy.47.dif_ref = f32[8,32,3,128]{3,2,1,0:T(4,128)} copy(f32[8,32,3,128]{3,1,2,0:T(8,128)S(1)} %copy-done.4) | data formatting | bytes 786432 | tf_op args[13]
  10.8 0.0 copy-done.6
  10.8 0.7 %copy.43.normals_ref = f32[64,3,128]{2,1,0:T(4,128)} copy(f32[64,3,128]{2,0,1:T(8,128)S(1)} %copy-done.6) | data formatting | bytes 196608 | tf_op args[5]
  11.5 0.0 copy-done.8
  11.5 0.7 %copy.44.inv_ref = f32[32,3,128]{2,1,0:T(4,128)} copy(f32[32,3,128]{2,0,1:T(8,128)S(1)} %copy-done.8) | data formatting | bytes 98304 | tf_op args[10]
  12.1 0.0 copy-done.9
  12.1 0.7 %copy.45.disp_ref = f32[32,3,128]{2,1,0:T(4,128)} copy(f32[32,3,128]{2,0,1:T(8,128)S(1)} %copy-done.9) | data formatting | bytes 98304 | tf_op args[11]
  12.8 41.3 %shard_map.157 = (bf16[5,320,128]{2,1,0:T(8,128)(2,1)}, bf16[5,320,128]{2,1,0:T(8,128)(2,1)}, f32[32,3,128]{2,1,0:T(4,128)}, f32[64,3,128]{2,1,0:T(4,128)}) custom-call(f32[4,8,384]{2,1,0:T(8,128)} %select_maximum_fusion.wall_ref, bf16[5,320,128]{2,1,0:T(8,128)(2,1)} %pad_maximum_fusion.prim_ref, f32[64,3,128]{2,1,0:T(4,128)} %copy.43.normals_ref, ...), custom_call_target="tpu_custom_call" | custom-call | tf_op jit(solution)/shard_map/pallas_call | solution.py:389
  54.1 0.0 copy-start.5
  54.1 0.0 copy-start.7
  54.1 4.6 %shard_map.158 = f32[5,1,320,128]{3,2,1,0:T(8,128)} custom-call(f32[1,320,128]{2,1,0:T(8,128)} %dens_ref.1, f32[3,1,320,128]{3,2,1,0:T(8,128)} %vel_ref.1, f32[1,320,128]{2,1,0:T(8,128)} %press_ref.1, bf16[5,320,128]{2,1,0:T(8,128)(2,1)} %get-tuple-element.7.low_ref, bf16[5,320,128]{2,1,0:T(8,128)(2,1)} %get-tuple-element.8.high_ref), custom_call_target="tpu_custom_call" | custom-call | tf_op jit(solution)/shard_map/pallas_call | solution.py:434
  58.7 0.0 copy-done.5
  58.7 0.6 %copy.49 = f32[64,3,128]{2,0,1:T(8,128)} copy(f32[64,3,128]{2,1,0:T(4,128)S(1)} %copy-done.5) | data formatting | bytes 196608
  59.4 0.0 copy-done.7
  59.4 0.6 %copy.48 = f32[32,3,128]{2,0,1:T(8,128)} copy(f32[32,3,128]{2,1,0:T(4,128)S(1)} %copy-done.7) | data formatting | bytes 98304
  (9 shorter events, 0.1 us)
Async XLA Ops:
  0.6 7.1 %copy-start = (f32[3,1,320,128]{3,2,1,0:T(8,128)S(1)}, f32[3,1,320,128]{3,2,1,0:T(8,128)}, u32[]{:S(2)}) copy-start(f32[3,1,320,128]{3,2,1,0:T(8,128)} %vel_ref.1) | copy-start | bytes 1474564
  0.6 7.1 %copy-start.1 = (f32[1,320,128]{2,1,0:T(8,128)S(1)}, f32[1,320,128]{2,1,0:T(8,128)}, u32[]{:S(2)}) copy-start(f32[1,320,128]{2,1,0:T(8,128)} %dens_ref.1) | copy-start | bytes 491524
  0.7 7.1 %copy-start.2 = (f32[1,320,128]{2,1,0:T(8,128)S(1)}, f32[1,320,128]{2,1,0:T(8,128)}, u32[]{:S(2)}) copy-start(f32[1,320,128]{2,1,0:T(8,128)} %press_ref.1) | copy-start | bytes 491524
  0.7 4.6 %copy-start.11 = (s32[64,1]{0,1:T(1,128)S(1)}, s32[64,1]{0,1:T(1,128)}, u32[]{:S(2)}) copy-start(s32[64,1]{0,1:T(1,128)} %param.20) | copy-start | bytes 772
  0.7 4.8 %copy-start.10 = (s32[64]{0:T(128)S(1)}, s32[64]{0:T(128)}, u32[]{:S(2)}) copy-start(s32[64]{0:T(128)} %param.21) | copy-start | bytes 772
  3.2 5.4 %copy-start.3 = (f32[8,32,3,128]{3,1,2,0:T(8,128)S(1)}, f32[8,32,3,128]{3,1,2,0:T(8,128)}, u32[]{:S(2)}) copy-start(f32[8,32,3,128]{3,1,2,0:T(8,128)} %param.26) | copy-start | bytes 1179652
  4.3 5.3 %copy-start.4 = (f32[8,32,3,128]{3,1,2,0:T(8,128)S(1)}, f32[8,32,3,128]{3,1,2,0:T(8,128)}, u32[]{:S(2)}) copy-start(f32[8,32,3,128]{3,1,2,0:T(8,128)} %param.27) | copy-start | bytes 1179652
  4.5 6.2 %copy-start.6 = (f32[64,3,128]{2,0,1:T(8,128)S(1)}, f32[64,3,128]{2,0,1:T(8,128)}, u32[]{:S(2)}) copy-start(f32[64,3,128]{2,0,1:T(8,128)} %param.19) | copy-start | bytes 294916
  6.4 5.1 %copy-start.8 = (f32[32,3,128]{2,0,1:T(8,128)S(1)}, f32[32,3,128]{2,0,1:T(8,128)}, u32[]{:S(2)}) copy-start(f32[32,3,128]{2,0,1:T(8,128)} %param.24) | copy-start | bytes 147460
  7.7 4.4 %copy-start.9 = (f32[32,3,128]{2,0,1:T(8,128)S(1)}, f32[32,3,128]{2,0,1:T(8,128)}, u32[]{:S(2)}) copy-start(f32[32,3,128]{2,0,1:T(8,128)} %param.25) | copy-start | bytes 147460
  54.1 4.7 %copy-start.5 = (f32[64,3,128]{2,1,0:T(4,128)S(1)}, f32[64,3,128]{2,1,0:T(4,128)}, u32[]{:S(2)}) copy-start(f32[64,3,128]{2,1,0:T(4,128)} %get-tuple-element.19) | copy-start | bytes 294916
  54.1 5.3 %copy-start.7 = (f32[32,3,128]{2,1,0:T(4,128)S(1)}, f32[32,3,128]{2,1,0:T(4,128)}, u32[]{:S(2)}) copy-start(f32[32,3,128]{2,1,0:T(4,128)} %get-tuple-element.18) | copy-start | bytes 147460

commit v3 on v2

--- a/solution.py
+++ b/solution.py
@@ -80,6 +80,59 @@
         result = advance(mid, (x_low, x_high), (y_low, y_high), (z_low, z_high))
         for i in range(5):
             out_ref[i, 0, rows, :] = result[i]
+
+
+def prepare_kernel(
+    capacity,
+    dens_ref,
+    vel_ref,
+    press_ref,
+    owner_ref,
+    owner_row_ref,
+    target_ref,
+    ends_ref,
+    prim_ref,
+    pick_ref,
+    place_ref,
+    tags_ref,
+    column,
+):
+    height, lanes = dens_ref.shape[1:]
+    fields = [dens_ref.at[0]] + [vel_ref.at[i, 0] for i in range(3)] + [press_ref.at[0]]
+    ends_ref[...] = jnp.ones_like(ends_ref)
+    column[...] = jnp.ones_like(column)
+    for i, field in enumerate(fields):
+        value = field[...]
+        prim_ref[i] = value.astype(jnp.bfloat16)
+        column[0:height, :] = value
+        for start in range(0, column.shape[0], lanes):
+            turned = column[start : start + lanes, :].T
+            for z in range(2):
+                ends_ref[z, i : i + 1, start : start + lanes] = turned[z : z + 1, :]
+    edge = ends_ref[0]
+    total = edge.shape[1]
+    lane = lax.broadcasted_iota(jnp.int32, edge.shape, 1)
+    ends_ref[2] = jnp.where(lane == height - 1, edge[:, 0:1], pltpu.roll(edge, total - 1, 1))
+    ends_ref[3] = jnp.where(lane == 0, edge[:, height - 1 : height], pltpu.roll(edge, 1, 1))
+
+    blocks, slot_count = pick_ref.shape
+    owner, owner_row = owner_ref[...], owner_row_ref[...]
+    row_id = lax.broadcasted_iota(jnp.int32, (blocks, blocks), 0)
+    column_id = lax.broadcasted_iota(jnp.int32, (blocks, blocks), 1)
+    same = jnp.where(owner == owner_row, 1.0, 0.0)
+    rank = jnp.sum(jnp.where(column_id < row_id, same, 0.0), axis=1, keepdims=True)
+    rank_row = jnp.sum(jnp.where(row_id < column_id, same, 0.0), axis=0, keepdims=True)
+    slot = owner.astype(jnp.float32) * capacity + rank
+    slot_row = owner_row.astype(jnp.float32) * capacity + rank_row
+    lane_id = lax.broadcasted_iota(jnp.int32, (blocks, slot_count), 1).astype(jnp.float32)
+    pick_ref[...] = jnp.where(slot == lane_id, 1.0, 0.0).astype(jnp.bfloat16)
+    line_id = lax.broadcasted_iota(jnp.int32, (slot_count, blocks), 0).astype(jnp.float32)
+    placed = jnp.where(slot_row == line_id, 1.0, 0.0)
+    place_ref[...] = placed.astype(jnp.bfloat16)
+    tag = jnp.sum(placed * (target_ref[...].astype(jnp.float32) + 1.0), axis=1, keepdims=True)
+    tag = jnp.broadcast_to(tag - 1.0, (slot_count, tags_ref.shape[2]))
+    for p in range(tags_ref.shape[0]):
+        tags_ref[p] = tag[p * capacity : (p + 1) * capacity, :]
 
 
 def thirds(value):
@@ -144,7 +197,7 @@
 ):
     me = lax.axis_index("group") * width + lax.axis_index("dev")
     blocks = index_ref.shape[0]
-    count = disp_ref.shape[0]
+    count = disp_ref.shape[1]
     columns = res_ref.shape[0]
     capacity = tags_ref.shape[1]
     nodes = index_ref.shape[1]
@@ -162,6 +215,12 @@
         return carry
 
     lax.fori_loop(1, peers, greet, 0)
+    products[...] = jnp.zeros_like(products)
+    for m in range(columns):
+        for n in range(m, columns):
+            line = jnp.sum(jnp.sum(res_ref[m] * res_ref[n], axis=0), axis=0, keepdims=True)
+            products[m * columns + n : m * columns + n + 1, :] = line
+            products[n * columns + m : n * columns + m + 1, :] = line
     pl.semaphore_wait(barrier, peers - 1)
 
     def near(slot, src, dst, distance):
@@ -176,7 +235,8 @@
 
     wall_up = near(0, wall_ref.at[0], side_ref.at[0], 1)
     wall_down = near(1, wall_ref.at[0], side_ref.at[1], peers - 1)
-    prior = near(2, disp_ref.at[count - 1], prior_ref, 1)
+    tail = prior_ref.shape[1]
+    prior = near(2, disp_ref.at[:, pl.ds(count - tail, tail), :], prior_ref, 1)
     bulk_up = near(3, prim_ref, low_ref, 1)
     bulk_down = near(4, prim_ref, high_ref, peers - 1)
 
@@ -213,16 +273,7 @@
     wall_down.start()
     prior.start()
     spread(tags_ref, tag_in, tag_send, tag_recv, True)
-    bulk_up.start()
-    bulk_down.start()
     tag_in[me] = tags_ref[me]
-
-    products[...] = jnp.zeros_like(products)
-    for m in range(columns):
-        for n in range(m, columns):
-            line = jnp.sum(jnp.sum(res_ref[m] * res_ref[n], axis=0), axis=0, keepdims=True)
-            products[m * columns + n : m * columns + n + 1, :] = line
-            products[n * columns + m : n * columns + m + 1, :] = line
 
     wall_up.wait()
     wall_down.wait()
@@ -245,9 +296,10 @@
         source = jnp.broadcast_to(wall[:, part * nodes : (part + 1) * nodes], index.shape)
         taken = jnp.take_along_axis(source, low, axis=1)
         found = jnp.where(index // nodes == part, taken, found)
-    slots[0:blocks, 0:nodes] = found
+    for c in range(3):
+        loads[:, c, :] = found * normals_ref[c]
     for b in range(blocks):
-        weighted = (slots[b : b + 1, 0:nodes] * normals_ref[b]).astype(jnp.bfloat16)
+        weighted = loads[b, 0:3, :].astype(jnp.bfloat16)
         loads[b, 0:3, :] = jnp.dot(weighted, rbf_ref[b], preferred_element_type=jnp.float32)
     spans = [slice(c * nodes, (c + 1) * nodes) for c in range(3)]
     for c in range(3):
@@ -255,13 +307,17 @@
     for p in range(peers):
         load_out[p] = slots[p * capacity : (p + 1) * capacity, :]
     spread(load_out, load_in, load_send, load_recv, True)
+    bulk_up.start()
+    bulk_down.start()
     load_in[me] = load_out[me]
 
     prior.wait()
     first = (me > 0).astype(jnp.float32)
-    for t in range(count):
-        half = disp_ref[t].astype(jnp.bfloat16)
-        earlier = disp_ref[t - 1] if t else prior_ref[...] * first
+    for c in range(3):
+        solid[:, c, :] = disp_ref[c]
+    for t in range(count - 1, -1, -1):
+        half = solid[t, 0:3, :].astype(jnp.bfloat16)
+        earlier = solid[t - 1, 0:3, :] if t else prior_ref[:, tail - 1, :] * first
         part = lax.dot_general(half, stiff_ref[t], LAST, preferred_element_type=jnp.float32)
         part = part + lax.dot_general(
             earlier.astype(jnp.bfloat16), coup_ref[t], LAST, preferred_element_type=jnp.float32
@@ -281,17 +337,19 @@
     gather(load_out, load_in, load_send, load_recv, True)
     for p in range(peers):
         slots[p * capacity : (p + 1) * capacity, :] = load_in[p]
-    for c in range(3):
-        solid[:, c, :] = solid[:, c, :] - select_rows(collector, slots[:, spans[c]])
-    change = -inv_ref[...] * solid[:, 0:3, :]
+    change = [
+        -inv_ref[c] * (solid[:, c, :] - select_rows(collector, slots[:, spans[c]]))
+        for c in range(3)
+    ]
     for m in range(columns):
-        line = jnp.sum(jnp.sum(res_ref[m] * change, axis=0), axis=0, keepdims=True)
+        line = sum(res_ref[m, c] * change[c] for c in range(3))
         at = columns * columns + m
-        products[at : at + 1, :] = line
+        products[at : at + 1, :] = jnp.sum(line, axis=0, keepdims=True)
     stat_out[...] = jnp.sum(products[...].T, axis=0, keepdims=True)
     spread(stat_out, stat_in, stat_send, stat_recv, False)
     stat_in[me] = stat_out[...]
-    solid[:, 0:3, :] = disp_ref[...] + change
+    for c in range(3):
+        next_ref[c] = disp_ref[c] + change[c]
     gather(stat_out, stat_in, stat_send, stat_recv, False)
     total = jnp.sum(stat_in[...], axis=0)
     shape = (columns, nodes)
@@ -306,14 +364,14 @@
         scaled = line / matrix[k : k + 1, k : k + 1]
         matrix = jnp.where(m_id == k, scaled, matrix - matrix[:, k : k + 1] * scaled)
     mixing = -matrix[:, columns : columns + 1]
-    result = solid[:, 0:3, :]
-    for m in range(columns):
-        result = result + dif_ref[m] * mixing[m : m + 1, :].reshape(1, 1, 1)
-    next_ref[...] = result
-    solid[:, 0:3, :] = result
-    for c in range(3):
-        rows = solid[:, c, :].astype(jnp.bfloat16)
-        slots[:, spans[c]] = jnp.dot(chooser, rows, preferred_element_type=jnp.float32)
+    for c in range(3):
+        result = next_ref[c]
+        for m in range(columns):
+            result = result + dif_ref[m, c] * mixing[m : m + 1, :]
+        next_ref[c] = result
+        slots[:, spans[c]] = jnp.dot(
+            chooser, result.astype(jnp.bfloat16), preferred_element_type=jnp.float32
+        )
     for p in range(peers):
         reply_out[p] = slots[p * capacity : (p + 1) * capacity, :].astype(jnp.bfloat16)
     spread(reply_out, reply_in, reply_send, reply_recv, True)
@@ -326,11 +384,17 @@
         loads[:, c, :] = jnp.dot(pick_ref[...], rows, preferred_element_type=jnp.float32)
     for b in range(blocks):
         reply = loads[b, 0:3, :].astype(jnp.bfloat16)
-        motion_ref[b] = lax.dot_general(
+        loads[b, 0:3, :] = lax.dot_general(
             reply, rbf_ref[b], LAST, preferred_element_type=jnp.float32
         )
+    for c in range(3):
+        motion_ref[c] = loads[:, c, :]
     bulk_up.wait()
     bulk_down.wait()
+
+
+def rows_last(value):
+    return jnp.swapaxes(value, -3, -2)
 
 
 def on_device(
@@ -359,46 +423,38 @@
     capacity = max(2, 2 * blocks // peers)
     slot_count = peers * capacity
 
-    ends = jnp.concatenate([density[None], velocity, pressure[None]], axis=0)[:, 0, :, 0:2]
-    ends = jnp.transpose(ends, (2, 0, 1))
-    ends = jnp.stack(
-        [ends[0], ends[1], jnp.roll(ends[0], -1, axis=1), jnp.roll(ends[0], 1, axis=1)]
-    )
-    padded = -(-height // nodes) * nodes
-    ends = jnp.pad(ends, ((0, 0), (0, 3), (0, padded - height)), constant_values=1.0)
-    prim = jnp.concatenate([density, velocity[:, 0], pressure], axis=0).astype(bf16)
-
-    owner = routes[:, 0]
-    same = (owner[:, None] == owner[None, :]) & (
-        jnp.arange(blocks)[:, None] > jnp.arange(blocks)[None, :]
-    )
-    slot_id = owner * capacity + jnp.sum(same.astype(jnp.int32), axis=1)
-    chosen = slot_id[:, None] == jnp.arange(slot_count, dtype=jnp.int32)[None, :]
-    pick = chosen.astype(bf16)
-    put = (jnp.arange(slot_count, dtype=jnp.int32)[:, None] == slot_id[None, :])
-    tag = jnp.sum(jnp.where(chosen, targets[:, None] + 1, 0), axis=0) - 1
-    tags = jnp.broadcast_to(
-        tag.astype(f32).reshape(peers, capacity)[:, :, None], (peers, capacity, nodes)
-    )
-
+    padded = -(-height // depth) * depth
+    halo = jax.ShapeDtypeStruct((5, height, depth), bf16)
     vmem = pl.BlockSpec(memory_space=pltpu.VMEM)
     anywhere = pl.BlockSpec(memory_space=pl.ANY)
     dma = pltpu.SemaphoreType.DMA
-    halo = jax.ShapeDtypeStruct((5, height, depth), bf16)
+    ends, prim, pick, put, tags = pl.pallas_call(
+        functools.partial(prepare_kernel, capacity),
+        out_shape=(
+            jax.ShapeDtypeStruct((4, 8, padded), f32),
+            halo,
+            jax.ShapeDtypeStruct((blocks, slot_count), bf16),
+            jax.ShapeDtypeStruct((slot_count, blocks), bf16),
+            jax.ShapeDtypeStruct((peers, capacity, nodes), f32),
+        ),
+        in_specs=[vmem] * 6,
+        out_specs=(vmem,) * 5,
+        scratch_shapes=[pltpu.VMEM((padded, depth), f32)],
+    )(density, velocity, pressure, routes, routes.reshape(1, blocks), targets.reshape(1, blocks))
     width_row = 3 * nodes
     low, high, disp_next, wall_motion = pl.pallas_call(
         functools.partial(couple_kernel, peers, width),
         out_shape=(
             halo,
             halo,
-            jax.ShapeDtypeStruct(displacement.shape, f32),
-            jax.ShapeDtypeStruct(normals.shape, f32),
+            jax.ShapeDtypeStruct((3, count, nodes), f32),
+            jax.ShapeDtypeStruct((3, blocks, nodes), f32),
         ),
         in_specs=[vmem, anywhere] + [vmem] * 12,
         out_specs=(anywhere, anywhere, vmem, vmem),
         scratch_shapes=[
             pltpu.VMEM((2, 8, padded), f32),
-            pltpu.VMEM((3, nodes), f32),
+            pltpu.VMEM((3, 8, nodes), f32),
             pltpu.VMEM((peers, capacity, nodes), f32),
             pltpu.VMEM((peers, capacity, width_row), f32),
             pltpu.VMEM((peers, capacity, width_row), f32),
@@ -418,18 +474,18 @@
     )(
         ends,
         prim,
-        normals,
+        rows_last(normals),
         correlation,
         rbf_blocks,
         pick,
-        put.astype(bf16),
+        put,
         tags,
         stiffness,
         coupling,
-        inverse_diag,
-        displacement,
-        diff_res,
-        diff_disp,
+        rows_last(inverse_diag),
+        rows_last(displacement),
+        rows_last(diff_res),
+        rows_last(diff_disp),
     )
     fluid_next = pl.pallas_call(
         flow_kernel,
@@ -437,7 +493,7 @@
         in_specs=[vmem] * 5,
         out_specs=vmem,
     )(density, velocity, pressure, low, high)
-    return (fluid_next, disp_next, wall_motion)
+    return (fluid_next, rows_last(disp_next), rows_last(wall_motion))
 
 
 def solution(mesh):

time: 60.2 us -> 49.8 us (0.83)
  local copies, waits for them, and re-layouts: 10.1 us -> 2.61 us
  other arithmetic: 3.17 us -> 0 us
    unnamed x34 -> x7, local copies, waits for them, and re-layouts: 9.11 us -> 2.61 us
    pallas_call x0 -> x1, Pallas kernels: none -> 2.24 us  [on_device(): pl.pallas_call(functools.partial(prepare_kernel, capacity), out_shape=(ja...]
    pallas_call x1, Pallas kernels: 41.3 us -> 39.5 us  [on_device(): pl.pallas_call(functools.partial(couple_kernel, peers, width), out_shape=...]
    convert_element_type x3 -> x0, other arithmetic: 1.31 us -> none  [the longest x1 0.68 us: on_device(): pick = chosen.astype(bf16)]
    concatenate x1 -> x0, other arithmetic: 0.79 us -> none  [on_device(): jnp.concatenate([density, velocity[:, 0], pressure], axis=0).astype(bf16)]
    broadcast_in_dim x1 -> x0, local copies, waits for them, and re-layouts: 0.74 us -> none  [on_device(): jnp.broadcast_to(tag.astype(f32).reshape(peers, capacity)[:, :, None], (p...]
    another operation x4 -> x0, other arithmetic: 0.73 us -> none  [the longest x2 0.71 us: on_device(): jnp.stack([ends[0], ends[1], jnp.roll(ends[0], -1, axis=1), jnp.roll(ends...]
where the time goes in v3:
time: 49.8 us; the launch traced here: 49.6 us
  Pallas kernels  46.4 us (93%)
  local copies, waits for them, and re-layouts  2.61 us (5%)
  between operations  0.66 us (1%)
    pallas_call x1, Pallas kernels, on_device(): pl.pallas_call(functools.partial(couple_kernel, peers, width), out_shape=...  39.5 us
    pallas_call x1, Pallas kernels, on_device(): pl.pallas_call(flow_kernel, out_shape=jax.ShapeDtypeStruct((5,) + density...  4.63 us
    unnamed x7, local copies, waits for them, and re-layouts  2.61 us
    pallas_call x1, Pallas kernels, on_device(): pl.pallas_call(functools.partial(prepare_kernel, capacity), out_shape=(ja...  2.24 us

profile of v3, /device:TPU:0, one launch (start us, length us, event | category | flops | bytes accessed | tf_op | source)
XLA Modules:
  0.0 49.6 jit_solution(95907866338312703)
XLA Ops:
  0.6 1.3 %copy.17.owner_ref = s32[64,1]{1,0:T(8,128)} copy(s32[64,1]{0,1:T(1,128)} %param.20) | data formatting | bytes 512 | tf_op args[6]
  2.0 2.2 %shard_map.157 = (f32[4,8,384]{2,1,0:T(8,128)}, bf16[5,320,128]{2,1,0:T(8,128)(2,1)}, bf16[64,128]{1,0:T(8,128)(2,1)}, bf16[128,64]{1,0:T(8,128)(2,1)}, f32[32,4,128]{2,1,0:T(4,128)}) custom-call(f32[1,320,128]{2,1,0:T(8,128)} %dens_ref.3, f32[3,1,320,128]{3,2,1,0:T(8,128)} %vel_ref.3, f32[1,320,128]{2,1,0:T(8,128)} %press_ref.3, s32[64,1]{1,0:T(8,128)} %copy.17.owner_ref, ...), custom_call_target="tpu_custom_call" | custom-call | tf_op jit(solution)/shard_map/pallas_call | solution.py:431
  4.2 39.5 %shard_map.158 = (bf16[5,320,128]{2,1,0:T(8,128)(2,1)}, bf16[5,320,128]{2,1,0:T(8,128)(2,1)}, f32[3,32,128]{2,1,0:T(8,128)}, f32[3,64,128]{2,1,0:T(8,128)}) custom-call(f32[4,8,384]{2,1,0:T(8,128)} %get-tuple-element.12.wall_ref, bf16[5,320,128]{2,1,0:T(8,128)(2,1)} %get-tuple-element.13.prim_ref, f32[3,64,128]{2,1,0:T(8,128)} %bitcast.12, ...), custom_call_target="tpu_custom_call" | custom-call | tf_op jit(solution)/shard_map/pallas_call | solution.py:445
  43.7 0.0 copy-start.1
  43.7 0.0 copy-start
  43.7 4.6 %shard_map.159 = f32[5,1,320,128]{3,2,1,0:T(8,128)} custom-call(f32[1,320,128]{2,1,0:T(8,128)} %dens_ref.3, f32[3,1,320,128]{3,2,1,0:T(8,128)} %vel_ref.3, f32[1,320,128]{2,1,0:T(8,128)} %press_ref.3, bf16[5,320,128]{2,1,0:T(8,128)(2,1)} %get-tuple-element.17.low_ref, bf16[5,320,128]{2,1,0:T(8,128)(2,1)} %get-tuple-element.18.high_ref), custom_call_target="tpu_custom_call" | custom-call | tf_op jit(solution)/shard_map/pallas_call | solution.py:490
  48.4 0.0 copy-done.1
  48.4 0.6 %copy.20 = f32[32,3,128]{2,0,1:T(8,128)} copy(f32[32,3,128]{2,0,1:T(8,128)S(1)} %bitcast.15) | data formatting | bytes 98304
  49.0 0.0 copy-done
  49.0 0.6 %copy.21 = f32[64,3,128]{2,0,1:T(8,128)} copy(f32[64,3,128]{2,0,1:T(8,128)S(1)} %bitcast.11) | data formatting | bytes 196608
Async XLA Ops:
  43.7 4.7 %copy-start.1 = (f32[3,32,128]{2,1,0:T(8,128)S(1)}, f32[3,32,128]{2,1,0:T(8,128)}, u32[]{:S(2)}) copy-start(f32[3,32,128]{2,1,0:T(8,128)} %get-tuple-element.19) | copy-start | bytes 147460
  43.7 5.3 %copy-start = (f32[3,64,128]{2,1,0:T(8,128)S(1)}, f32[3,64,128]{2,1,0:T(8,128)}, u32[]{:S(2)}) copy-start(f32[3,64,128]{2,1,0:T(8,128)} %get-tuple-element.20) | copy-start | bytes 294916

commit v4 on v3

--- a/solution.py
+++ b/solution.py
@@ -167,10 +167,14 @@
     disp_ref,
     res_ref,
     dif_ref,
+    dens_ref,
+    vel_ref,
+    press_ref,
+    fluid_ref,
+    next_ref,
+    motion_ref,
     low_ref,
     high_ref,
-    next_ref,
-    motion_ref,
     side_ref,
     prior_ref,
     tag_in,
@@ -237,8 +241,15 @@
     wall_down = near(1, wall_ref.at[0], side_ref.at[1], peers - 1)
     tail = prior_ref.shape[1]
     prior = near(2, disp_ref.at[:, pl.ds(count - tail, tail), :], prior_ref, 1)
-    bulk_up = near(3, prim_ref, low_ref, 1)
-    bulk_down = near(4, prim_ref, high_ref, peers - 1)
+    early, late = pl.ds(0, 3), pl.ds(3, 2)
+    bulk_early = (
+        near(3, prim_ref.at[early], low_ref.at[early], 1),
+        near(4, prim_ref.at[early], high_ref.at[early], peers - 1),
+    )
+    bulk_late = (
+        near(5, prim_ref.at[late], low_ref.at[late], 1),
+        near(6, prim_ref.at[late], high_ref.at[late], peers - 1),
+    )
 
     def spread(src, dst, send, recv, indexed):
         def begin(step, carry):
@@ -273,6 +284,8 @@
     wall_down.start()
     prior.start()
     spread(tags_ref, tag_in, tag_send, tag_recv, True)
+    for copy in bulk_early:
+        copy.start()
     tag_in[me] = tags_ref[me]
 
     wall_up.wait()
@@ -307,8 +320,6 @@
     for p in range(peers):
         load_out[p] = slots[p * capacity : (p + 1) * capacity, :]
     spread(load_out, load_in, load_send, load_recv, True)
-    bulk_up.start()
-    bulk_down.start()
     load_in[me] = load_out[me]
 
     prior.wait()
@@ -347,6 +358,8 @@
         products[at : at + 1, :] = jnp.sum(line, axis=0, keepdims=True)
     stat_out[...] = jnp.sum(products[...].T, axis=0, keepdims=True)
     spread(stat_out, stat_in, stat_send, stat_recv, False)
+    for copy in bulk_late:
+        copy.start()
     stat_in[me] = stat_out[...]
     for c in range(3):
         next_ref[c] = disp_ref[c] + change[c]
@@ -376,6 +389,9 @@
         reply_out[p] = slots[p * capacity : (p + 1) * capacity, :].astype(jnp.bfloat16)
     spread(reply_out, reply_in, reply_send, reply_recv, True)
     reply_in[me] = reply_out[me]
+    for copy in bulk_early + bulk_late:
+        copy.wait()
+    flow_kernel(dens_ref, vel_ref, press_ref, low_ref, high_ref, fluid_ref)
     gather(reply_out, reply_in, reply_send, reply_recv, True)
     for p in range(peers):
         slots[p * capacity : (p + 1) * capacity, :] = reply_in[p].astype(jnp.float32)
@@ -389,8 +405,6 @@
         )
     for c in range(3):
         motion_ref[c] = loads[:, c, :]
-    bulk_up.wait()
-    bulk_down.wait()
 
 
 def rows_last(value):
@@ -442,17 +456,18 @@
         scratch_shapes=[pltpu.VMEM((padded, depth), f32)],
     )(density, velocity, pressure, routes, routes.reshape(1, blocks), targets.reshape(1, blocks))
     width_row = 3 * nodes
-    low, high, disp_next, wall_motion = pl.pallas_call(
+    fluid_next, disp_next, wall_motion = pl.pallas_call(
         functools.partial(couple_kernel, peers, width),
         out_shape=(
-            halo,
-            halo,
+            jax.ShapeDtypeStruct((5,) + density.shape, f32),
             jax.ShapeDtypeStruct((3, count, nodes), f32),
             jax.ShapeDtypeStruct((3, blocks, nodes), f32),
         ),
-        in_specs=[vmem, anywhere] + [vmem] * 12,
-        out_specs=(anywhere, anywhere, vmem, vmem),
+        in_specs=[vmem, anywhere] + [vmem] * 15,
+        out_specs=(vmem, vmem, vmem),
         scratch_shapes=[
+            pltpu.VMEM(halo.shape, bf16),
+            pltpu.VMEM(halo.shape, bf16),
             pltpu.VMEM((2, 8, padded), f32),
             pltpu.VMEM((3, 8, nodes), f32),
             pltpu.VMEM((peers, capacity, nodes), f32),
@@ -466,8 +481,8 @@
             pltpu.VMEM((slot_count, width_row), f32),
             pltpu.VMEM((count, 8, nodes), f32),
             pltpu.VMEM((nodes, nodes), f32),
-            dma((5,)),
-            dma((5,)),
+            dma((7,)),
+            dma((7,)),
         ]
         + [dma((peers,))] * 8,
         compiler_params=pltpu.CompilerParams(collective_id=0, has_side_effects=True),
@@ -486,13 +501,10 @@
         rows_last(displacement),
         rows_last(diff_res),
         rows_last(diff_disp),
+        density,
+        velocity,
+        pressure,
     )
-    fluid_next = pl.pallas_call(
-        flow_kernel,
-        out_shape=jax.ShapeDtypeStruct((5,) + density.shape, f32),
-        in_specs=[vmem] * 5,
-        out_specs=vmem,
-    )(density, velocity, pressure, low, high)
     return (fluid_next, rows_last(disp_next), rows_last(wall_motion))
 
 

time: 49.8 us -> 48.5 us (0.974)
  Pallas kernels: 46.4 us -> 41.2 us
  local copies, waits for them, and re-layouts: 2.61 us -> 6.4 us
    pallas_call x1 -> x0, Pallas kernels: 4.63 us -> none  [on_device(): pl.pallas_call(flow_kernel, out_shape=jax.ShapeDtypeStruct((5,) + density...]
    unnamed x7 -> x4, local copies, waits for them, and re-layouts: 2.61 us -> 6.4 us
where the time goes in v4:
time: 48.5 us; the launch traced here: 48.3 us
  Pallas kernels  41.2 us (85%)
  local copies, waits for them, and re-layouts  6.4 us (13%)
  between operations  0.64 us (1%)
    pallas_call x1, Pallas kernels, on_device(): pl.pallas_call(functools.partial(couple_kernel, peers, width), out_shape=...  39 us
    unnamed x4, local copies, waits for them, and re-layouts  6.4 us
    pallas_call x1, Pallas kernels, on_device(): pl.pallas_call(functools.partial(prepare_kernel, capacity), out_shape=(ja...  2.24 us

profile of v4, /device:TPU:0, one launch (start us, length us, event | category | flops | bytes accessed | tf_op | source)
XLA Modules:
  0.0 48.3 jit_solution(11180928725654042596)
XLA Ops:
  0.6 1.3 %copy.17.owner_ref = s32[64,1]{1,0:T(8,128)} copy(s32[64,1]{0,1:T(1,128)} %param.20) | data formatting | bytes 512 | tf_op args[6]
  2.0 2.2 %shard_map.157 = (f32[4,8,384]{2,1,0:T(8,128)}, bf16[5,320,128]{2,1,0:T(8,128)(2,1)}, bf16[64,128]{1,0:T(8,128)(2,1)}, bf16[128,64]{1,0:T(8,128)(2,1)}, f32[32,4,128]{2,1,0:T(4,128)}) custom-call(f32[1,320,128]{2,1,0:T(8,128)} %dens_ref.3, f32[3,1,320,128]{3,2,1,0:T(8,128)} %vel_ref.3, f32[1,320,128]{2,1,0:T(8,128)} %press_ref.3, s32[64,1]{1,0:T(8,128)} %copy.17.owner_ref, ...), custom_call_target="tpu_custom_call" | custom-call | tf_op jit(solution)/shard_map/pallas_call | solution.py:445
  4.2 39.0 %shard_map.158 = (f32[5,1,320,128]{3,2,1,0:T(8,128)}, f32[3,32,128]{2,1,0:T(8,128)}, f32[3,64,128]{2,1,0:T(8,128)}) custom-call(f32[4,8,384]{2,1,0:T(8,128)} %get-tuple-element.11.wall_ref, bf16[5,320,128]{2,1,0:T(8,128)(2,1)} %get-tuple-element.12.prim_ref, f32[3,64,128]{2,1,0:T(8,128)} %bitcast.12, s32[64,128]{1,0:T(8,128)} %index_ref.1, ...), custom_call_target="tpu_custom_call" | custom-call | tf_op jit(solution)/shard_map/pallas_call | solution.py:459
  43.2 2.1 %copy.21 = f32[5,1,320,128]{3,2,1,0:T(8,128)} copy(f32[5,1,320,128]{3,2,1,0:T(8,128)} %get-tuple-element.22) | data formatting | bytes 1638400
  45.3 1.4 %copy.22 = f32[32,3,128]{2,0,1:T(8,128)} copy(f32[32,3,128]{2,0,1:T(8,128)} %bitcast.15) | data formatting | bytes 98304
  46.7 1.5 %copy.23 = f32[64,3,128]{2,0,1:T(8,128)} copy(f32[64,3,128]{2,0,1:T(8,128)} %bitcast.11) | data formatting | bytes 196608
